TPU v7x, 512 devices: a whole 4x8x8 slice. The times are simulated.
512 devices in a mesh: seq: 8 (over z), vocab: 64 (over y, x, core).
Axes of the slice: x: 4, y: 8, z: 8, core: 2. Of those that a mesh axis runs over, the one named last changes fastest.
Arguments:
- hidden: bfloat16 [2048, 8192], P('seq', 'vocab'), may hold values from -120 to 120
- head_weight: bfloat16 [8192, 98304], P('seq', 'vocab'), may hold values from -0.0625 to 0.0625
- vocab_basis: bfloat16 [98304, 1024], P('vocab', 'seq'), may hold values from -0.0048828125 to 0.0048828125
- keep_index: int32 [512], P('seq'), may hold values from 0 to 255, as said below
- counts: int32 [8], P('seq'), may hold values from 1 to 64, as said below
Outputs:
- coefficients: float32 [512, 1024], P('seq', 'vocab')
Inputs may be any that keep to these rules, and one draw needn't show every extreme that they name: `keep_index`: each owner's list is strictly increasing and ends at 255. `counts`: exactly one owner has all 64 slots live.
All inputs are finite; a program needn't handle non-finite values.
Results may differ from a plain program's by a relative error of at most 0.0032.
Values may be sent and summed in bfloat16 or wider, within the bound.
No kernel may reach another device: no remote copies, remote signals or barrier semaphores. Data moves between devices by JAX's collectives and lax.ppermute only.
A program may use at most 64 MiB of HBM per device.

v0:
```python
import jax
import jax.numpy as jnp
from jax import lax
from jax.sharding import PartitionSpec as P


def shards(hidden, head_weight, vocab_basis, keep_index, counts):
    chosen = jnp.take(hidden, keep_index, axis=0)
    features = lax.all_gather(chosen, "vocab", axis=1, tiled=True)
    pieces = lax.all_to_all(features, "seq", split_axis=1, concat_axis=0, tiled=True)
    owned = features.shape[0]
    logits = lax.psum_scatter(
        jnp.dot(pieces, head_weight, preferred_element_type=jnp.float32),
        "seq",
        scatter_dimension=0,
        tiled=True,
    )
    row_max = lax.pmax(jnp.max(logits, axis=1, keepdims=True), "vocab")
    weights = jnp.exp(logits - row_max)
    denominator, weighted = lax.psum(
        (jnp.sum(weights, axis=1, keepdims=True), jnp.sum(weights * logits, axis=1, keepdims=True)),
        "vocab",
    )
    expected = weighted / denominator
    centred = (logits - expected).astype(jnp.bfloat16)
    partial_sums = jnp.dot(
        centred,
        lax.all_gather(vocab_basis, "seq", axis=1, tiled=True),
        preferred_element_type=jnp.float32,
    )
    summed = lax.psum_scatter(partial_sums, "vocab", scatter_dimension=1, tiled=True)
    live_rows = jnp.arange(owned, dtype=jnp.int32) < counts[0]
    return jnp.where(live_rows[:, None], summed, jnp.float32(0.0))


def solution(mesh):
    in_specs = (P("seq", "vocab"), P("seq", "vocab"), P("vocab", "seq"), P("seq"), P("seq"))
    out_specs = P("seq", "vocab")
    return jax.shard_map(shards, mesh=mesh, in_specs=in_specs, out_specs=out_specs, check_vma=False)
```

profile of v0, /device:TPU:1, one launch (start us, length us, event | category | flops | bytes accessed | tf_op | source)
XLA Modules:
  0.0 629.1 jit_solution(8558448056872284931)
XLA Ops:
  6.5 0.0 copy-start
  6.5 0.0 all-gather.3.cloned.1.call-start
  6.5 0.8 compare_select_fusion
  7.3 0.8 compare_and_fusion
  8.2 1.5 gather_fusion
  9.6 0.7 broadcast_select_fusion
  10.3 0.0 all-gather.3.cloned.1.call-update
  10.3 0.0 reduce-scatter.2.cloned.1.call-start
  10.4 81.5 %all-gather.3.cloned.1.call-done = bf16[64,8192]{1,0:T(8,128)(2,1)} async-done(((bf16[64,128]{1,0:T(8,128)(2,1)}), bf16[64,8192]{1,0:T(8,128)(2,1)}) %all-gather.3.cloned.1.call-update) | async-done | bytes 1048592 | tf_op jit(solution)/shard_map/all_gather | solution.py:9
  91.9 1.3 copy.10
  93.2 35.5 %all_to_all.19 = bf16[64,8,1024]{2,0,1:T(8,128)(2,1)S(1)} all-to-all(bf16[64,8,1024]{2,0,1:T(8,128)(2,1)S(1)} %bitcast.17), channel_id=1, replica_groups=mesh['seq'=8,'vocab'=64] {'seq'}, dimensions={1} | all-to-all | bytes 2097152 | tf_op jit(solution)/shard_map/all_to_all | solution.py:10
  128.6 0.0 copy-done
  128.6 3.5 fusion.3
  132.1 0.0 reduce-scatter.2.cloned.1.call-update
  132.2 0.0 all-gather.5.cloned.1.call-start
  132.2 0.7 all-gather.5.cloned.1.call-update
  132.9 0.0 all-reduce.4.cloned.1.call-start
  133.0 41.2 %reduce-scatter.2.cloned.1.call-done = f32[64,1536]{1,0:T(8,128)} async-done(((f32[512,1536]{1,0:T(8,128)}), f32[64,1536]{1,0:T(8,128)}) %reduce-scatter.2.cloned.1.call-update) | async-done | bytes 393232 | tf_op jit(solution)/shard_map/reduce_scatter | solution.py:12
  174.1 1.1 reduce_max.9
  175.2 127.0 %pmax.7 = f32[64]{0:T(128)S(1)} all-reduce(f32[64]{0:T(128)S(1)} %reduce_max.9), channel_id=1, replica_groups=mesh['seq'=8,'vocab'=64] {'vocab'}, use_global_device_ids=true, to_apply=%region_2.3 | all-reduce | flops 64 | bytes 512 | tf_op jit(solution)/shard_map/pmax | solution.py:18
  302.2 1.2 fusion
  303.4 125.6 %all-reduce.1 = (f32[64,1]{0,1:T(1,128)S(1)}, f32[64,1]{0,1:T(1,128)S(1)}) all-reduce(f32[64,1]{0,1:T(1,128)S(1)} %bitcast.21, f32[64,1]{0,1:T(1,128)S(1)} %bitcast.20), channel_id=1, replica_groups=mesh['seq'=8,'vocab'=64] {'vocab'}, use_global_device_ids=true, to_apply=%region_4.5 | all-reduce | flops 128 | bytes 1024 | tf_op jit(solution)/shard_map/psum | solution.py:20
  429.0 0.0 all-gather.5.cloned.1.call-done
  429.0 4.2 fusion.1
  433.2 0.0 all-reduce.4.cloned.1.call-update
  433.9 1.3 dynamic-slice
  435.8 185.4 %all-reduce.4.cloned.1.call-done = f32[64,1024]{0,1:T(8,128)} async-done(((f32[64,1024]{0,1:T(8,128)}), f32[64,1024]{0,1:T(8,128)}) %all-reduce.4.cloned.1.call-update) | async-done | bytes 262160
  621.3 1.3 dynamic-slice_select_fusion
  (3 shorter events, 0.0 us)
Async XLA Ops:
  6.5 122.1 %copy-start = (bf16[1024,1536]{1,0:T(8,128)(2,1)S(1)}, bf16[1024,1536]{1,0:T(8,128)(2,1)}, u32[]{:S(2)}) copy-start(bf16[1024,1536]{1,0:T(8,128)(2,1)} %param.6) | copy-start | bytes 9437188
  6.5 85.3 %all-gather.3.cloned.1.call-start = ((), (), s32[]{:S(2)}) async-start(), calls=%async_computation.2 | async-start | bytes 1064960 | tf_op jit(solution)/shard_map/all_gather | solution.py:9
  10.3 163.8 %reduce-scatter.2.cloned.1.call-start = ((), (), s32[]{:S(2)}) async-start(), calls=%async_computation.3 | async-start | bytes 3538944 | tf_op jit(solution)/shard_map/reduce_scatter | solution.py:12
  132.2 296.9 %all-gather.5.cloned.1.call-start = ((), (), s32[]{:S(2)}) async-start(), calls=%async_computation.4 | async-start | bytes 3538944 | tf_op jit(solution)/shard_map/all_gather | solution.py:28
  132.9 488.4 %all-reduce.4.cloned.1.call-start = ((), (), s32[]{:S(2)}) async-start(), calls=%async_computation.5 | async-start | bytes 1048576
Sparse Core Ops, SparseCore 0:
  10.6 81.2 all-gather.2
  132.3 41.7 reduce-scatter.1
  176.1 56.0 all-gather.4
  433.4 187.8 all-reduce.3
where the time goes:
time: 630 us; the launch traced here: 629 us
  waiting for transfers between devices  309 us (49%)
  blocking collectives  288 us (46%)
  between operations  14.5 us (2%)
  matrix products  7.68 us (1%)
    unnamed x5, waiting for transfers between devices  186 us
    pmax x1, blocking collectives, shards(): row_max = lax.pmax(jnp.max(logits, axis=1, keepdims=True), 'vocab')  127 us
    psum x1, blocking collectives, shards(): lax.psum((jnp.sum(weights, axis=1, keepdims=True), jnp.sum(weights * logi...  126 us
    all_gather x1, waiting for transfers between devices, shards(): features = lax.all_gather(chosen, 'vocab', axis=1, tiled=True)  81.5 us
    reduce_scatter x1, waiting for transfers between devices, shards(): lax.psum_scatter(jnp.dot(pieces, head_weight, preferred_element_type=jnp....  41.2 us
    all_to_all x1, blocking collectives, shards(): lax.all_to_all(features, 'seq', split_axis=1, concat_axis=0, tiled=True)  35.5 us
  transfers between devices with their start and end apart: 4, of which 3 were waited for; matrix products, arithmetic and copies ran while one was open for 1% of the time, Pallas kernels for 0%

commit v1 on v0

v1 whole, which is shorter than its diff:
```python
import jax
import jax.numpy as jnp
from jax import lax
from jax.experimental import pallas as pl
from jax.experimental.pallas import tpu as pltpu
from jax.sharding import Mesh, PartitionSpec as P

F32 = jnp.float32
BF16 = jnp.bfloat16
Z = ("zh", "zl")
ALL = ("zh", "zl", "y", "x", "c")
VMEM = pl.BlockSpec(memory_space=pltpu.VMEM)
SMEM = pl.BlockSpec(memory_space=pltpu.SMEM)


def call(kernel, out_shape, in_specs, *args, scratch=()):
    multi = isinstance(out_shape, (list, tuple))
    return pl.pallas_call(
        kernel,
        out_shape=out_shape,
        in_specs=in_specs,
        out_specs=[VMEM] * len(out_shape) if multi else VMEM,
        scratch_shapes=list(scratch),
    )(*args)


def select_kernel(index_ref, hidden_ref, out_ref):
    rows = lax.broadcasted_iota(jnp.int32, (256, 64), 0)
    chosen = jnp.where(rows == index_ref[...], 1.0, 0.0).astype(BF16)
    picked = lax.dot_general(
        chosen, hidden_ref[...], (((0,), (0,)), ((), ())), preferred_element_type=F32
    ).astype(BF16)
    for i in range(8):
        out_ref[i] = picked


def logits_kernel(core_ref, own_ref, other_ref, head_ref, out_ref):
    first = core_ref[0] == 0
    for half in range(2):
        rows = pl.ds(half * 256, 256)
        features = []
        for x in range(4):
            own, other = own_ref[x, rows, :], other_ref[x, rows, :]
            features.append(jnp.where(first, own, other))
            features.append(jnp.where(first, other, own))
        lhs = jnp.concatenate(features, axis=1)
        for n in range(6):
            part = jnp.dot(
                lhs, head_ref[:, n * 256 : (n + 1) * 256], preferred_element_type=F32
            ).astype(BF16)
            for t in range(2):
                tile = 2 * n + t
                lanes = pl.ds((tile % 3) * 128, 128)
                out_ref[half * 4 + tile // 3, :, lanes] = part[:, t * 128 : (t + 1) * 128]


def project_kernel(core_ref, parts_ref, basis_ref, keep_ref, send_ref, cols_ref, extra_ref):
    core = core_ref[0]
    logits = parts_ref[0].astype(F32)
    for i in range(1, 8):
        logits = logits + parts_ref[i].astype(F32)
    top = jnp.max(logits, axis=1, keepdims=True)
    weights = jnp.exp(logits - top)
    denominator = jnp.sum(weights, axis=1, keepdims=True)
    weighted = jnp.sum(weights * logits, axis=1, keepdims=True)
    lane = lax.broadcasted_iota(jnp.int32, (256, 128), 1)
    stats = jnp.where(lane == 0, top, jnp.where(lane == 1, denominator, jnp.where(lane == 2, weighted, 0.0)))
    extra_ref[...] = stats.T[0:8, :]
    high = logits.astype(BF16)
    low = (logits - high.astype(F32)).astype(BF16)
    lhs = jnp.concatenate([high, low, jnp.ones((16, 384), BF16)], axis=0)
    for j in range(4):
        rhs = jnp.concatenate([basis_ref[2 * j], basis_ref[2 * j + 1]], axis=1)
        both = jnp.dot(lhs, rhs, preferred_element_type=F32)
        turned = (both[0:256] + both[256:512]).T
        extra_ref[4 + j : 5 + j, :] = both[512:513]
        for y in range(2):
            for x in range(4):
                for c in range(2):
                    start = y * 128 + x * 32 + c * 16
                    cols_ref[c, x, 2 * j + y] = turned[start : start + 16]
    keep_ref[0:512, :] = cols_ref[core].reshape(512, 256)
    send_ref[0:512, :] = cols_ref[1 - core].reshape(512, 256)
    keep_ref[512:520, :] = extra_ref[...]
    send_ref[512:520, :] = extra_ref[...]


def combine(extras):
    top = extras[0][0:1]
    for e in extras[1:]:
        top = jnp.maximum(top, e[0:1])
    row = lax.broadcasted_iota(jnp.int32, extras[0].shape, 0)
    total = None
    for e in extras:
        scaled = jnp.where(row < 3, e * jnp.exp(e[0:1] - top), e)
        total = scaled if total is None else total + scaled
    return jnp.where(row == 0, top, total)


def core_kernel(keep_ref, recv_ref, out_ref):
    extra = combine([keep_ref[512:520, :], recv_ref[512:520, :]])
    for x in range(4):
        rows = pl.ds(x * 128, 128)
        out_ref[x, 0:128, :] = keep_ref[rows, :] + recv_ref[rows, :]
        out_ref[x, 128:136, :] = extra


def x_kernel(in_ref, out_ref):
    extra = combine([in_ref[i, 128:136, :] for i in range(4)])
    for y in range(8):
        rows = pl.ds(y * 16, 16)
        out_ref[y, 0:16, :] = (in_ref[0, rows, :] + in_ref[1, rows, :]) + (in_ref[2, rows, :] + in_ref[3, rows, :])
        out_ref[y, 16:24, :] = extra


def y_kernel(place_ref, in_ref, out_ref):
    extra = combine([in_ref[i, 16:24, :] for i in range(8)])
    total = in_ref[0, 0:16, :]
    for i in range(1, 8):
        total = total + in_ref[i, 0:16, :]
    row = lax.broadcasted_iota(jnp.int32, (8, 256), 0)
    line = jnp.sum(jnp.where(row == 4 + place_ref[0], extra, 0.0), axis=0, keepdims=True)
    lane = lax.broadcasted_iota(jnp.int32, (16, 256), 1)
    sub = lax.broadcasted_iota(jnp.int32, (16, 256), 0)
    sums = jnp.sum(jnp.where(lane == sub + place_ref[1], line, 0.0), axis=1, keepdims=True)
    low = lax.broadcasted_iota(jnp.int32, (16, 128), 1) < 64
    for o in range(4):
        lanes = slice((o // 2) * 128, (o // 2) * 128 + 128)
        block, stats = total[:, lanes], extra[:, lanes]
        if o % 2:
            block, stats = pltpu.roll(block, 64, 1), pltpu.roll(stats, 64, 1)
        out_ref[o, 0:16, :] = jnp.where(low, block, sums)
        out_ref[o, 16:24, :] = stats


def finish_kernel(count_ref, in_ref, out_ref):
    total = in_ref[0, 0:16, :]
    for i in range(1, 4):
        total = total + in_ref[i, 0:16, :]
    stats = combine([in_ref[i, 16:24, :] for i in range(4)])
    expected = stats[2:3] / stats[1:2]
    result = total - expected * total[:, 64:65]
    lane = lax.broadcasted_iota(jnp.int32, (16, 128), 1)
    result = jnp.where(lane < count_ref[0], result, 0.0)
    out_ref[...] = result.T[0:64, :]


def shards(hidden, head_weight, vocab_basis, keep_index, counts):
    def shape(*dims, dtype=F32):
        return jax.ShapeDtypeStruct(dims, dtype)

    def exchange(v, axes):
        return lax.all_to_all(v, axes, 0, 0, tiled=True)

    def swap(v):
        return lax.ppermute(v, "c", [(0, 1), (1, 0)])

    core = lax.axis_index("c").astype(jnp.int32)
    column = lax.axis_index("y") * 128 + lax.axis_index("x") * 32 + core * 16
    place = jnp.stack([column // 256, column % 256]).astype(jnp.int32)
    core = core.reshape(1)

    owned = call(select_kernel, shape(8, 64, 128, dtype=BF16), [VMEM, VMEM], keep_index.reshape(1, 64), hidden)
    sliced = exchange(exchange(owned, "y"), Z)
    basis_parts = jnp.broadcast_to(vocab_basis.reshape(1, 4, 384, 128), (2, 4, 384, 128)).reshape(8, 384, 128)
    basis = exchange(basis_parts, Z)
    mine = exchange(jnp.broadcast_to(sliced.reshape(1, 512, 128), (4, 512, 128)), "x")
    theirs = swap(mine)
    parts = call(
        logits_kernel, shape(8, 256, 384, dtype=BF16), [SMEM, VMEM, VMEM, VMEM], core, mine, theirs, head_weight
    )
    parts = exchange(parts, Z)
    keep, send = call(
        project_kernel,
        [shape(520, 256), shape(520, 256)],
        [SMEM, VMEM, VMEM],
        core,
        parts,
        basis,
        scratch=[pltpu.VMEM((2, 4, 8, 16, 256), F32), pltpu.VMEM((8, 256), F32)],
    )
    sums = call(core_kernel, shape(4, 136, 256), [VMEM, VMEM], keep, swap(send))
    sums = call(x_kernel, shape(8, 24, 256), [VMEM], exchange(sums, "x"))
    sums = call(y_kernel, shape(4, 24, 128), [SMEM, VMEM], place, exchange(sums, "y"))
    return call(finish_kernel, shape(64, 16), [SMEM, VMEM], counts, exchange(sums, "zl"))


def solution(mesh):
    grid = Mesh(mesh.devices.reshape(2, 4, 8, 4, 2), ALL)
    rows, cols = ("zh", "zl"), ("y", "x", "c")
    in_specs = (P(rows, cols), P(rows, cols), P(cols, rows), P(rows), P(rows))
    return jax.shard_map(shards, mesh=grid, in_specs=in_specs, out_specs=P(rows, cols), check_vma=False)
```

time: 630 us -> 169 us (0.27)
  waiting for transfers between devices: 309 us -> 19.8 us
  blocking collectives: 288 us -> 96.4 us
  starting transfers between devices: 0.12 us -> 25.5 us
  Pallas kernels: 0 us -> 17.6 us
  between operations: 14.5 us -> 0.74 us
  matrix products: 7.68 us -> 0 us
    unnamed x5 -> x0, waiting for transfers between devices: 186 us -> none
    pmax x1 -> x0, blocking collectives: 127 us -> none  [shards(): row_max = lax.pmax(jnp.max(logits, axis=1, keepdims=True), 'vocab')]
    psum x1 -> x0, blocking collectives: 126 us -> none  [shards(): lax.psum((jnp.sum(weights, axis=1, keepdims=True), jnp.sum(weights * logi...]
    all_gather x2 -> x0, waiting for transfers between devices: 81.5 us -> none  [the longest x1 81.5 us: shards(): features = lax.all_gather(chosen, 'vocab', axis=1, tiled=True)]
    all_to_all x1 -> x5, blocking collectives: 35.5 us -> 96.4 us  [exchange(): return lax.all_to_all(v, axes, 0, 0, tiled=True)]
    reduce_scatter x1 -> x0, waiting for transfers between devices: 41.2 us -> none  [shards(): lax.psum_scatter(jnp.dot(pieces, head_weight, preferred_element_type=jnp....]
    pallas_call x0 -> x7, Pallas kernels: none -> 17.6 us  [call(): pl.pallas_call(kernel, out_shape=out_shape, in_specs=in_specs, out_specs=...]
    all_to_all x0 -> x3, waiting for transfers between devices: none -> 16.5 us  [exchange(): return lax.all_to_all(v, axes, 0, 0, tiled=True)]
  transfers between devices with their start and end apart: 4 -> 5, of which waited for: 3 -> 5; matrix products, arithmetic and copies ran while one was open for 1% -> 0% of each run, Pallas kernels for 0% -> 3%
where the time goes in v1:
time: 169 us; the launch traced here: 166 us
  blocking collectives  96.4 us (57%)
  starting transfers between devices  25.5 us (15%)
  waiting for transfers between devices  19.8 us (12%)
  Pallas kernels  17.6 us (10%)
  local copies, waits for them, and re-layouts  5.47 us (3%)
    all_to_all x5, blocking collectives, exchange(): return lax.all_to_all(v, axes, 0, 0, tiled=True)  96.4 us
    pallas_call x7, Pallas kernels, call(): pl.pallas_call(kernel, out_shape=out_shape, in_specs=in_specs, out_specs=...  17.6 us
    all_to_all x3, waiting for transfers between devices, exchange(): return lax.all_to_all(v, axes, 0, 0, tiled=True)  16.5 us
    ppermute x2, starting transfers between devices, swap(): return lax.ppermute(v, 'c', [(0, 1), (1, 0)])  15.3 us
    all_to_all x3, starting transfers between devices, exchange(): return lax.all_to_all(v, axes, 0, 0, tiled=True)  10.2 us
  transfers between devices with their start and end apart: 5, of which 5 were waited for; matrix products, arithmetic and copies ran while one was open for 0% of the time, Pallas kernels for 3%

profile of v1, /device:TPU:1, one launch (start us, length us, event | category | flops | bytes accessed | tf_op | source)
XLA Modules:
  0.0 166.1 jit_solution(11336612557232707233)
XLA Ops:
  0.0 1.8 %shard_map.55 = bf16[8,64,128]{2,1,0:T(8,128)(2,1)} custom-call(s32[1,64]{1,0:T(1,128)} %bitcast.9, bf16[256,128]{1,0:T(8,128)(2,1)} %hidden_ref.1), custom_call_target="tpu_custom_call" | custom-call | tf_op jit(solution)/shard_map/pallas_call | solution.py:18
  1.8 15.7 %all_to_all.40 = bf16[8,64,128]{2,1,0:T(8,128)(2,1)S(1)} all-to-all(bf16[8,64,128]{2,1,0:T(8,128)(2,1)} %shard_map.55), channel_id=1, replica_groups=mesh['zh'=2,'zl'=4,'y'=8,'x'=4,'c'=2] {'y'}, dimensions={0} | all-to-all | bytes 262144 | tf_op jit(solution)/shard_map/all_to_all | solution.py:153
  17.4 17.5 %all_to_all.41 = bf16[8,64,128]{2,1,0:T(8,128)(2,1)S(1)} all-to-all(bf16[8,64,128]{2,1,0:T(8,128)(2,1)S(1)} %all_to_all.40), channel_id=1, replica_groups=mesh['zh'=2,'zl'=4,'y'=8,'x'=4,'c'=2] {'zh','zl'}, dimensions={0} | all-to-all | bytes 262144 | tf_op jit(solution)/shard_map/all_to_all | solution.py:153
  34.9 0.1 broadcast_in_dim.15
  35.0 10.7 %all_to_all.42.own_ref = bf16[4,512,128]{2,1,0:T(8,128)(2,1)S(1)} all-to-all(bf16[4,512,128]{2,1,0:T(8,128)(2,1)S(1)} %broadcast_in_dim.15), channel_id=1, replica_groups=mesh['zh'=2,'zl'=4,'y'=8,'x'=4,'c'=2] {'x'}, dimensions={0} | all-to-all | bytes 1048576 | tf_op jit(solution)/shard_map/all_to_all | solution.py:153
  45.7 0.0 copy-done.5
  45.7 1.1 broadcast_in_dim.17
  46.8 3.5 %all-to-all-start.4 = ((bf16[8,384,128]{2,1,0:T(8,128)(2,1)}), bf16[8,384,128]{2,1,0:T(8,128)(2,1)S(1)}, u32[]{:S(2)}, u32[]{:S(2)}) async-start(bf16[8,384,128]{2,1,0:T(8,128)(2,1)} %bitcast.6), calls=%async_computation.4 | async-start | bytes 1572864 | tf_op jit(solution)/shard_map/all_to_all | solution.py:153
  50.3 7.0 %collective-permute-start = (bf16[4,512,128]{2,1,0:T(8,128)(2,1)S(1)}, bf16[4,512,128]{2,1,0:T(8,128)(2,1)S(1)}, u32[]{:S(2)}, u32[]{:S(2)}) collective-permute-start(bf16[4,512,128]{2,1,0:T(8,128)(2,1)S(1)} %all_to_all.42.own_ref), channel_id=1, source_target_pairs={{0,1},{1,0},{2,3},{3,2},{4,5},{5,4},{6,7},{7,6},{8,9},{9,8},{10,11... | collective-permute-start | bytes 1572872 | tf_op jit(solution)/shard_map/ppermute | solution.py:156
  57.4 1.5 collective-permute-done.other_ref
  58.9 0.0 copy-done.1
  58.9 0.8 copy-done.4
  59.7 5.2 %shard_map.56 = bf16[8,256,384]{2,1,0:T(8,128)(2,1)} custom-call(s32[1]{0:T(128)} %bitcast.2.core_ref, bf16[4,512,128]{2,1,0:T(8,128)(2,1)} %copy-done.1, bf16[4,512,128]{2,1,0:T(8,128)(2,1)} %copy-done.4, bf16[1024,1536]{1,0:T(8,128)(2,1)} %head_ref.1), custom_call_target="tpu_custom_call" | custom-call | tf_op jit(solution)/shard_map/pallas_call | solution.py:18
  64.9 4.9 %all-to-all-done.4.basis_ref = bf16[8,384,128]{2,1,0:T(8,128)(2,1)S(1)} async-done(((bf16[8,384,128]{2,1,0:T(8,128)(2,1)}), bf16[8,384,128]{2,1,0:T(8,128)(2,1)S(1)}, u32[]{:S(2)}, u32[]{:S(2)}) %all-to-all-start.4) | async-done | bytes 786464 | tf_op jit(solution)/shard_map/all_to_all | solution.py:153
  69.8 38.9 %all_to_all.43.parts_ref = bf16[8,256,384]{2,1,0:T(8,128)(2,1)} all-to-all(bf16[8,256,384]{2,1,0:T(8,128)(2,1)} %shard_map.56), channel_id=1, replica_groups=mesh['zh'=2,'zl'=4,'y'=8,'x'=4,'c'=2] {'zh','zl'}, dimensions={0} | all-to-all | bytes 3145728 | tf_op jit(solution)/shard_map/all_to_all | solution.py:153
  108.7 3.6 %shard_map.57 = (f32[520,256]{1,0:T(8,128)}, f32[520,256]{1,0:T(8,128)}) custom-call(s32[1]{0:T(128)} %bitcast.2.core_ref, bf16[8,256,384]{2,1,0:T(8,128)(2,1)} %all_to_all.43.parts_ref, bf16[8,384,128]{2,1,0:T(8,128)(2,1)} %copy-done), custom_call_target="tpu_custom_call" | custom-call | tf_op jit(solution)/shard_map/pallas_call | solution.py:18
  112.3 8.2 %collective-permute-start.1 = (f32[520,256]{1,0:T(8,128)}, f32[520,256]{1,0:T(8,128)S(1)}, u32[]{:S(2)}, u32[]{:S(2)}) collective-permute-start(f32[520,256]{1,0:T(8,128)} %get-tuple-element.8), channel_id=1, source_target_pairs={{0,1},{1,0},{2,3},{3,2},{4,5},{5,4},{6,7},{7,6},{8,9},{9,8},{10,11... | collective-permute-start | bytes 1597448 | tf_op jit(solution)/shard_map/ppermute | solution.py:156
  120.5 1.7 %collective-permute-done.1.recv_ref = f32[520,256]{1,0:T(8,128)S(1)} collective-permute-done((f32[520,256]{1,0:T(8,128)}, f32[520,256]{1,0:T(8,128)S(1)}, u32[]{:S(2)}, u32[]{:S(2)}) %collective-permute-start.1) | collective-permute-done | bytes 532512 | tf_op jit(solution)/shard_map/ppermute | solution.py:156
  122.2 0.8 copy-done.3
  123.0 2.1 %shard_map.58 = f32[4,136,256]{2,1,0:T(8,128)} custom-call(f32[520,256]{1,0:T(8,128)} %get-tuple-element.7.keep_ref, f32[520,256]{1,0:T(8,128)} %copy-done.3), custom_call_target="tpu_custom_call" | custom-call | tf_op jit(solution)/shard_map/pallas_call | solution.py:18
  125.1 13.7 %all_to_all.44.in_ref = f32[4,136,256]{2,1,0:T(8,128)} all-to-all(f32[4,136,256]{2,1,0:T(8,128)} %shard_map.58), channel_id=1, replica_groups=mesh['zh'=2,'zl'=4,'y'=8,'x'=4,'c'=2] {'x'}, dimensions={0} | all-to-all | bytes 1114112 | tf_op jit(solution)/shard_map/all_to_all | solution.py:153
  138.8 1.8 %shard_map.59 = f32[8,24,256]{2,1,0:T(8,128)} custom-call(f32[4,136,256]{2,1,0:T(8,128)} %all_to_all.44.in_ref), custom_call_target="tpu_custom_call" | custom-call | tf_op jit(solution)/shard_map/pallas_call | solution.py:18
  140.5 3.4 %all-to-all-start.6 = ((f32[8,24,256]{2,1,0:T(8,128)}), f32[8,24,256]{2,1,0:T(8,128)S(1)}, u32[]{:S(2)}, u32[]{:S(2)}) async-start(f32[8,24,256]{2,1,0:T(8,128)} %shard_map.59), calls=%async_computation.6 | async-start | bytes 393216 | tf_op jit(solution)/shard_map/all_to_all | solution.py:153
  144.0 0.6 pad_add_fusion.place_ref
  144.6 7.8 %all-to-all-done.6.in_ref = f32[8,24,256]{2,1,0:T(8,128)S(1)} async-done(((f32[8,24,256]{2,1,0:T(8,128)}), f32[8,24,256]{2,1,0:T(8,128)S(1)}, u32[]{:S(2)}, u32[]{:S(2)}) %all-to-all-start.6) | async-done | bytes 196640 | tf_op jit(solution)/shard_map/all_to_all | solution.py:153
  152.4 0.7 copy-done.2
  153.0 1.7 %shard_map.60 = f32[4,24,128]{2,1,0:T(8,128)} custom-call(s32[2]{0:T(128)} %pad_add_fusion.place_ref, f32[8,24,256]{2,1,0:T(8,128)} %copy-done.2), custom_call_target="tpu_custom_call" | custom-call | tf_op jit(solution)/shard_map/pallas_call | solution.py:18
  154.7 3.3 %all-to-all-start.7 = ((f32[4,24,128]{2,1,0:T(8,128)}), f32[4,24,128]{2,1,0:T(8,128)S(1)}, u32[]{:S(2)}, u32[]{:S(2)}) async-start(f32[4,24,128]{2,1,0:T(8,128)} %shard_map.60), calls=%async_computation.7 | async-start | bytes 98304 | tf_op jit(solution)/shard_map/all_to_all | solution.py:153
  158.6 3.9 %all-to-all-done.7.in_ref = f32[4,24,128]{2,1,0:T(8,128)S(1)} async-done(((f32[4,24,128]{2,1,0:T(8,128)}), f32[4,24,128]{2,1,0:T(8,128)S(1)}, u32[]{:S(2)}, u32[]{:S(2)}) %all-to-all-start.7) | async-done | bytes 49184 | tf_op jit(solution)/shard_map/all_to_all | solution.py:153
  162.5 0.6 copy-done.6
  163.1 1.6 shard_map.61
  164.7 1.4 copy.6
  (8 shorter events, 0.0 us)
Async XLA Ops:
  0.0 45.7 %copy-start.5 = (bf16[1536,128]{1,0:T(8,128)(2,1)S(1)}, bf16[1536,128]{1,0:T(8,128)(2,1)}, u32[]{:S(2)}) copy-start(bf16[1536,128]{1,0:T(8,128)(2,1)} %param.7) | copy-start | bytes 1179652
  45.7 13.2 %copy-start.1 = (bf16[4,512,128]{2,1,0:T(8,128)(2,1)}, bf16[4,512,128]{2,1,0:T(8,128)(2,1)S(1)}, u32[]{:S(2)}) copy-start(bf16[4,512,128]{2,1,0:T(8,128)(2,1)S(1)} %all_to_all.42.own_ref) | copy-start | bytes 1572868
  46.8 23.0 %all-to-all-start.4 = ((bf16[8,384,128]{2,1,0:T(8,128)(2,1)}), bf16[8,384,128]{2,1,0:T(8,128)(2,1)S(1)}, u32[]{:S(2)}, u32[]{:S(2)}) async-start(bf16[8,384,128]{2,1,0:T(8,128)(2,1)} %bitcast.6), calls=%async_computation.4 | async-start | bytes 1572864 | tf_op jit(solution)/shard_map/all_to_all | solution.py:153
  50.3 8.6 %collective-permute-start = (bf16[4,512,128]{2,1,0:T(8,128)(2,1)S(1)}, bf16[4,512,128]{2,1,0:T(8,128)(2,1)S(1)}, u32[]{:S(2)}, u32[]{:S(2)}) collective-permute-start(bf16[4,512,128]{2,1,0:T(8,128)(2,1)S(1)} %all_to_all.42.own_ref), channel_id=1, source_target_pairs={{0,1},{1,0},{2,3},{3,2},{4,5},{5,4},{6,7},{7,6},{8,9},{9,8},{10,11... | collective-permute-start | bytes 1572872 | tf_op jit(solution)/shard_map/ppermute | solution.py:156
  58.9 0.8 copy-start.4
  69.8 38.9 %copy-start = (bf16[8,384,128]{2,1,0:T(8,128)(2,1)}, bf16[8,384,128]{2,1,0:T(8,128)(2,1)S(1)}, u32[]{:S(2)}) copy-start(bf16[8,384,128]{2,1,0:T(8,128)(2,1)S(1)} %all-to-all-done.4.basis_ref) | copy-start | bytes 2359300
  112.3 10.0 %collective-permute-start.1 = (f32[520,256]{1,0:T(8,128)}, f32[520,256]{1,0:T(8,128)S(1)}, u32[]{:S(2)}, u32[]{:S(2)}) collective-permute-start(f32[520,256]{1,0:T(8,128)} %get-tuple-element.8), channel_id=1, source_target_pairs={{0,1},{1,0},{2,3},{3,2},{4,5},{5,4},{6,7},{7,6},{8,9},{9,8},{10,11... | collective-permute-start | bytes 1597448 | tf_op jit(solution)/shard_map/ppermute | solution.py:156
  122.2 0.8 copy-start.3
  140.5 11.8 %all-to-all-start.6 = ((f32[8,24,256]{2,1,0:T(8,128)}), f32[8,24,256]{2,1,0:T(8,128)S(1)}, u32[]{:S(2)}, u32[]{:S(2)}) async-start(f32[8,24,256]{2,1,0:T(8,128)} %shard_map.59), calls=%async_computation.6 | async-start | bytes 393216 | tf_op jit(solution)/shard_map/all_to_all | solution.py:153
  152.3 0.7 copy-start.2
  154.7 7.8 %all-to-all-start.7 = ((f32[4,24,128]{2,1,0:T(8,128)}), f32[4,24,128]{2,1,0:T(8,128)S(1)}, u32[]{:S(2)}, u32[]{:S(2)}) async-start(f32[4,24,128]{2,1,0:T(8,128)} %shard_map.60), calls=%async_computation.7 | async-start | bytes 98304 | tf_op jit(solution)/shard_map/all_to_all | solution.py:153
  162.5 0.6 copy-start.6

commit v2 on v0

v2 whole, which is shorter than its diff:
```python
import jax
import jax.numpy as jnp
from jax import lax
from jax.experimental import pallas as pl
from jax.experimental.pallas import tpu as pltpu
from jax.sharding import Mesh, PartitionSpec as P


F32 = jnp.float32
BF16 = jnp.bfloat16
G = 4
LANES = 64 * G
PART = 1536 // G
Z = ("zh", "zl")
ALL = ("zh", "zl", "y", "x", "c")
VMEM = pl.BlockSpec(memory_space=pltpu.VMEM)
SMEM = pl.BlockSpec(memory_space=pltpu.SMEM)
OUTER = pl.BlockSpec(memory_space=pltpu.VMEM)
STAY = pl.BlockSpec(memory_space=pl.ANY)


def call(kernel, out_shape, in_specs, *args, scratch=(), out_memory=pltpu.VMEM):
    args = [
        pltpu.with_memory_space_constraint(a, pltpu.VMEM) if spec is VMEM else a
        for a, spec in zip(args, in_specs)
    ]
    return pl.pallas_call(
        kernel,
        out_shape=out_memory(*out_shape) if out_memory else jax.ShapeDtypeStruct(*out_shape),
        in_specs=in_specs,
        out_specs=VMEM,
        scratch_shapes=list(scratch),
    )(*args)


def split(v):
    high = v.astype(BF16)
    return high, (v - high.astype(F32)).astype(BF16)


def iota(shape, axis):
    return lax.broadcasted_iota(jnp.int32, shape, axis)


def select_kernel(index_ref, hidden_ref, out_ref):
    chosen = jnp.where(iota((256, 64), 0) == index_ref[...], 1.0, 0.0).astype(BF16)
    picked = lax.dot_general(
        chosen, hidden_ref[...], (((0,), (0,)), ((), ())), preferred_element_type=F32
    ).astype(BF16)
    for i in range(8):
        out_ref[i] = picked


def logits_kernel(core_ref, own_ref, other_ref, head_ref, out_ref, held_ref, sems):
    copies = [
        pltpu.make_async_copy(head_ref.at[:, pl.ds(n * 256, 256)], held_ref.at[n], sems.at[n]) for n in range(6)
    ]
    for copy in copies:
        copy.start()
    first = core_ref[0] == 0
    lhs = []
    for group in range(8 // G):
        rows = pl.ds(group * LANES, LANES)
        features = []
        for x in range(4):
            own, other = own_ref[x, rows, :], other_ref[x, rows, :]
            features.append(jnp.where(first, own, other))
            features.append(jnp.where(first, other, own))
        lhs.append(jnp.concatenate(features, axis=1))
    for n in range(6):
        copies[n].wait()
        for group in range(8 // G):
            part = jnp.dot(lhs[group], held_ref[n], preferred_element_type=F32).astype(BF16)
            for t in range(2):
                piece, lane = divmod((2 * n + t) * 128, PART)
                out_ref[group * G + piece, :, pl.ds(lane, 128)] = part[:, t * 128 : (t + 1) * 128]


def project_kernel(parts_ref, basis_ref, out_ref):
    logits = parts_ref[0].astype(F32)
    for i in range(1, 8):
        logits = logits + parts_ref[i].astype(F32)
    top_high, top_low = split(jnp.max(logits, axis=1, keepdims=True))
    top_high, top_low = top_high.astype(F32), top_low.astype(F32)
    weights = jnp.exp(logits - (top_high + top_low))
    den_high, den_low = split(jnp.sum(weights, axis=1, keepdims=True))
    wei_high, wei_low = split(jnp.sum(weights * logits, axis=1, keepdims=True))
    lane = iota((LANES, 128), 1)
    stats = jnp.zeros((LANES, 128), F32)
    for i, v in enumerate([top_high, top_low, den_high, den_low, wei_high, wei_low]):
        stats = jnp.where(lane == i, v.astype(F32), stats)
    stats = stats.T[0:16, :]
    high, low = split(logits)
    lhs = jnp.concatenate([high, low, jnp.ones((128, PART), BF16)], axis=0)
    lane = iota((16, 128), 1)
    spread = []
    for j in range(4):
        rhs = jnp.concatenate([basis_ref[2 * j], basis_ref[2 * j + 1]], axis=1)
        both = jnp.dot(lhs, rhs, preferred_element_type=F32)
        turned = (both[0:LANES] + both[LANES : 2 * LANES]).T.astype(BF16)
        sums = both[2 * LANES : 2 * LANES + 128].T
        for half in range(2):
            y = 2 * j + half
            line = jnp.zeros((16, 128), F32)
            for block in range(8):
                start = half * 128 + block * 16
                out_ref[block, y * 16 : y * 16 + 16, :] = turned[start : start + 16]
                line = jnp.where(lane == block, sums[start : start + 16], line)
            spread.append(line)
    sums = jnp.concatenate(spread, axis=0).T
    row = iota((16, LANES), 0)
    for block in range(8):
        sums_high, sums_low = split(sums[block : block + 1])
        extra = jnp.where(row < 6, stats, 0.0)
        if LANES > 128:
            zero = jnp.zeros((1, LANES - 128), BF16)
            sums_high = jnp.concatenate([sums_high, zero], axis=1)
            sums_low = jnp.concatenate([sums_low, zero], axis=1)
        extra = jnp.where(row == 6, sums_high.astype(F32), extra)
        extra = jnp.where(row == 7, sums_low.astype(F32), extra)
        out_ref[block, 128:144, :] = extra.astype(BF16)


def merge(tiles):
    tops = [t[0:1] + t[1:2] for t in tiles]
    top = tops[0]
    for t in tops[1:]:
        top = jnp.maximum(top, t)
    denominator, weighted, sums = 0.0, 0.0, 0.0
    for mine, tile in zip(tops, tiles):
        scale = jnp.exp(mine - top)
        denominator = denominator + scale * (tile[2:3] + tile[3:4])
        weighted = weighted + scale * (tile[4:5] + tile[5:6])
        sums = sums + (tile[6:7] + tile[7:8])
    return top, denominator, weighted, sums


def chip_kernel(in_ref, out_ref):
    total = in_ref[0, 0:128, :].astype(F32)
    for i in range(1, 8):
        total = total + in_ref[i, 0:128, :].astype(F32)
    top, denominator, weighted, sums = merge([in_ref[i, 128:144, :].astype(F32) for i in range(8)])
    pairs = [h for v in (top, denominator, weighted) for h in split(v)]
    sums_high, sums_low = split(sums[:, 0:128])
    sums_high, sums_low = sums_high.astype(F32), sums_low.astype(F32)
    row, lane = iota((16, 128), 0), iota((16, 128), 1)
    for owner in range(G):
        lanes = slice((owner // 2) * 128, (owner // 2) * 128 + 128)
        stats = jnp.zeros((16, 128), F32)
        for i, v in enumerate(pairs):
            stats = jnp.where(row == i, v[:, lanes].astype(F32), stats)
        if owner % 2 == 0:
            stats = pltpu.roll(stats, 64, 1)
        for y in range(8):
            block = total[y * 16 : y * 16 + 16, lanes]
            if owner % 2:
                block = pltpu.roll(block, 64, 1)
            shift = (64 - 16 * y) % 128
            line_high = pltpu.roll(jnp.broadcast_to(sums_high, (8, 128)), shift, 1)[0:1]
            line_low = pltpu.roll(jnp.broadcast_to(sums_low, (8, 128)), shift, 1)[0:1]
            extra = jnp.where(row == 6, line_high, jnp.where(row == 7, line_low, stats))
            out_ref[y * G + owner] = jnp.where(lane < 64, block, extra).astype(BF16)


def finish_kernel(count_ref, in_ref, out_ref):
    tiles = [in_ref[i].astype(F32) for i in range(8 * G)]
    total = tiles[0]
    for t in tiles[1:]:
        total = total + t
    _, denominator, weighted, sums = merge(tiles)
    expected = pltpu.roll(jnp.broadcast_to(weighted / denominator, (8, 128)), 64, 1)[0:1]
    row, lane = iota((16, 128), 0), iota((16, 128), 1)
    column = jnp.sum(jnp.where(lane == row + 64, sums, 0.0), axis=1, keepdims=True)
    result = jnp.where(lane < count_ref[0], total - expected * column, 0.0)
    out_ref[...] = result[:, 0:64]


def shards(hidden, head_weight, vocab_basis, keep_index, counts):
    def exchange(v, axes):
        return lax.all_to_all(v, axes, 0, 0, tiled=True)

    core = lax.axis_index("c").astype(jnp.int32).reshape(1)
    basis_parts = jnp.broadcast_to(vocab_basis.reshape(1, G, PART, 128), (8 // G, G, PART, 128))
    basis = exchange(basis_parts.reshape(8, PART, 128), Z)
    owned = call(select_kernel, ((8, 64, 128), BF16), [OUTER, OUTER], keep_index.reshape(1, 64), hidden)
    sliced = exchange(exchange(owned, "y"), Z)
    mine = exchange(jnp.broadcast_to(sliced.reshape(1, 512, 128), (4, 512, 128)), "x")
    theirs = lax.ppermute(mine, "c", [(0, 1), (1, 0)])
    parts = call(
        logits_kernel,
        ((8, LANES, PART), BF16),
        [SMEM, VMEM, VMEM, STAY],
        core,
        mine,
        theirs,
        head_weight,
        scratch=[pltpu.VMEM((6, 1024, 256), BF16), pltpu.SemaphoreType.DMA((6,))],
    )
    sums = call(project_kernel, ((8, 144, LANES), BF16), [VMEM, VMEM], exchange(parts, Z), basis)
    sums = call(chip_kernel, ((8 * G, 16, 128), BF16), [VMEM], exchange(sums, ("x", "c")))
    sums = exchange(sums, ("y", "zl"))
    return call(finish_kernel, ((16, 64), F32), [SMEM, VMEM], counts, sums, out_memory=None).T


def solution(mesh):
    grid = Mesh(mesh.devices.reshape(8 // G, G, 8, 4, 2), ALL)
    rows, cols = ("zh", "zl"), ("y", "x", "c")
    in_specs = (P(rows, cols), P(rows, cols), P(cols, rows), P(rows), P(rows))
    return jax.shard_map(shards, mesh=grid, in_specs=in_specs, out_specs=P(rows, cols), check_vma=False)
```

time: 630 us -> 144 us (0.23)
  waiting for transfers between devices: 309 us -> 18.1 us
  blocking collectives: 288 us -> 99.7 us
  starting transfers between devices: 0.12 us -> 15.1 us
  between operations: 14.5 us -> 0.71 us
  Pallas kernels: 0 us -> 8.63 us
  matrix products: 7.68 us -> 0 us
    unnamed x5 -> x0, waiting for transfers between devices: 186 us -> none
    pmax x1 -> x0, blocking collectives: 127 us -> none  [shards(): row_max = lax.pmax(jnp.max(logits, axis=1, keepdims=True), 'vocab')]
    psum x1 -> x0, blocking collectives: 126 us -> none  [shards(): lax.psum((jnp.sum(weights, axis=1, keepdims=True), jnp.sum(weights * logi...]
    all_gather x2 -> x0, waiting for transfers between devices: 81.5 us -> none  [the longest x1 81.5 us: shards(): features = lax.all_gather(chosen, 'vocab', axis=1, tiled=True)]
    all_to_all x1 -> x5, blocking collectives: 35.5 us -> 99.7 us  [exchange(): return lax.all_to_all(v, axes, 0, 0, tiled=True)]
    reduce_scatter x1 -> x0, waiting for transfers between devices: 41.2 us -> none  [shards(): lax.psum_scatter(jnp.dot(pieces, head_weight, preferred_element_type=jnp....]
    all_to_all x0 -> x2, waiting for transfers between devices: none -> 16.6 us  [exchange(): return lax.all_to_all(v, axes, 0, 0, tiled=True)]
    pallas_call x0 -> x5, Pallas kernels: none -> 8.63 us  [call(): pl.pallas_call(kernel, out_shape=out_memory(*out_shape) if out_memory els...]
  transfers between devices with their start and end apart: 4 -> 3, of which waited for: 3 -> 3; matrix products, arithmetic and copies ran while one was open for 1% -> 0% of each run, Pallas kernels for 0% -> 3%
where the time goes in v2:
time: 144 us; the launch traced here: 143 us
  blocking collectives  99.7 us (69%)
  waiting for transfers between devices  18.1 us (13%)
  starting transfers between devices  15.1 us (10%)
  Pallas kernels  8.63 us (6%)
    all_to_all x5, blocking collectives, exchange(): return lax.all_to_all(v, axes, 0, 0, tiled=True)  99.7 us
    all_to_all x2, waiting for transfers between devices, exchange(): return lax.all_to_all(v, axes, 0, 0, tiled=True)  16.6 us
    pallas_call x5, Pallas kernels, call(): pl.pallas_call(kernel, out_shape=out_memory(*out_shape) if out_memory els...  8.63 us
    all_to_all x2, starting transfers between devices, exchange(): return lax.all_to_all(v, axes, 0, 0, tiled=True)  8.06 us
    ppermute x1, starting transfers between devices, shards(): theirs = lax.ppermute(mine, 'c', [(0, 1), (1, 0)])  7.05 us
  transfers between devices with their start and end apart: 3, of which 3 were waited for; matrix products, arithmetic and copies ran while one was open for 0% of the time, Pallas kernels for 3%

profile of v2, /device:TPU:1, one launch (start us, length us, event | category | flops | bytes accessed | tf_op | source)
XLA Modules:
  0.0 143.3 jit_solution(9846033424803019067)
XLA Ops:
  0.0 0.0 copy-start
  0.0 1.1 shard_map.55
  1.1 15.4 %all_to_all.35 = bf16[8,64,128]{2,1,0:T(8,128)(2,1)S(1)} all-to-all(bf16[8,64,128]{2,1,0:T(8,128)(2,1)S(1)} %shard_map.55), channel_id=1, replica_groups=mesh['zh'=2,'zl'=4,'y'=8,'x'=4,'c'=2] {'y'}, dimensions={0} | all-to-all | bytes 262144 | tf_op jit(solution)/shard_map/all_to_all | solution.py:180
  16.5 17.6 %all_to_all.36 = bf16[8,64,128]{2,1,0:T(8,128)(2,1)S(1)} all-to-all(bf16[8,64,128]{2,1,0:T(8,128)(2,1)S(1)} %all_to_all.35), channel_id=1, replica_groups=mesh['zh'=2,'zl'=4,'y'=8,'x'=4,'c'=2] {'zh','zl'}, dimensions={0} | all-to-all | bytes 262144 | tf_op jit(solution)/shard_map/all_to_all | solution.py:180
  34.1 0.1 broadcast_in_dim.15
  34.1 10.7 %all_to_all.37.own_ref = bf16[4,512,128]{2,1,0:T(8,128)(2,1)S(1)} all-to-all(bf16[4,512,128]{2,1,0:T(8,128)(2,1)S(1)} %broadcast_in_dim.15), channel_id=1, replica_groups=mesh['zh'=2,'zl'=4,'y'=8,'x'=4,'c'=2] {'x'}, dimensions={0} | all-to-all | bytes 1048576 | tf_op jit(solution)/shard_map/all_to_all | solution.py:180
  44.9 0.0 copy-done
  44.9 1.0 broadcast_in_dim.17
  45.9 4.2 %all-to-all-start.4 = ((bf16[8,384,128]{2,1,0:T(8,128)(2,1)}), bf16[8,384,128]{2,1,0:T(8,128)(2,1)}, u32[]{:S(2)}, u32[]{:S(2)}) async-start(bf16[8,384,128]{2,1,0:T(8,128)(2,1)} %bitcast.4), calls=%async_computation.4 | async-start | bytes 1572864 | tf_op jit(solution)/shard_map/all_to_all | solution.py:180
  50.1 7.0 %collective-permute-start = (bf16[4,512,128]{2,1,0:T(8,128)(2,1)S(1)}, bf16[4,512,128]{2,1,0:T(8,128)(2,1)S(1)}, u32[]{:S(2)}, u32[]{:S(2)}) collective-permute-start(bf16[4,512,128]{2,1,0:T(8,128)(2,1)S(1)} %all_to_all.37.own_ref), channel_id=1, source_target_pairs={{0,1},{1,0},{2,3},{3,2},{4,5},{5,4},{6,7},{7,6},{8,9},{9,8},{10,11... | collective-permute-start | bytes 1572872 | tf_op jit(solution)/shard_map/ppermute | solution.py:188
  57.2 1.5 %collective-permute-done.other_ref = bf16[4,512,128]{2,1,0:T(8,128)(2,1)S(1)} collective-permute-done((bf16[4,512,128]{2,1,0:T(8,128)(2,1)S(1)}, bf16[4,512,128]{2,1,0:T(8,128)(2,1)S(1)}, u32[]{:S(2)}, u32[]{:S(2)}) %collective-permute-start) | collective-permute-done | bytes 524320 | tf_op jit(solution)/shard_map/ppermute | solution.py:188
  58.7 3.7 %shard_map.56 = bf16[8,256,384]{2,1,0:T(8,128)(2,1)S(1)} custom-call(s32[1]{0:T(128)} %bitcast.core_ref, bf16[4,512,128]{2,1,0:T(8,128)(2,1)S(1)} %all_to_all.37.own_ref, bf16[4,512,128]{2,1,0:T(8,128)(2,1)S(1)} %collective-permute-done.other_ref, bf16[1024,1536]{1,0:T(8,128)(2,1)} %head_ref.1), custom_call_target="tpu_custom_call" | custom-call | tf_op jit(solution)/shard_map/pallas_call | solution.py:27
  62.4 7.2 %all-to-all-done.4.basis_ref = bf16[8,384,128]{2,1,0:T(8,128)(2,1)} async-done(((bf16[8,384,128]{2,1,0:T(8,128)(2,1)}), bf16[8,384,128]{2,1,0:T(8,128)(2,1)}, u32[]{:S(2)}, u32[]{:S(2)}) %all-to-all-start.4) | async-done | bytes 786464 | tf_op jit(solution)/shard_map/all_to_all | solution.py:180
  69.6 37.0 %all_to_all.38.parts_ref = bf16[8,256,384]{2,1,0:T(8,128)(2,1)S(1)} all-to-all(bf16[8,256,384]{2,1,0:T(8,128)(2,1)S(1)} %shard_map.56), channel_id=1, replica_groups=mesh['zh'=2,'zl'=4,'y'=8,'x'=4,'c'=2] {'zh','zl'}, dimensions={0} | all-to-all | bytes 3145728 | tf_op jit(solution)/shard_map/all_to_all | solution.py:180
  106.7 2.2 %shard_map.57 = bf16[8,144,256]{2,1,0:T(8,128)(2,1)S(1)} custom-call(bf16[8,256,384]{2,1,0:T(8,128)(2,1)S(1)} %all_to_all.38.parts_ref, bf16[8,384,128]{2,1,0:T(8,128)(2,1)} %all-to-all-done.4.basis_ref), custom_call_target="tpu_custom_call" | custom-call | tf_op jit(solution)/shard_map/pallas_call | solution.py:27
  108.9 19.0 %all_to_all.39.in_ref = bf16[8,144,256]{2,1,0:T(8,128)(2,1)S(1)} all-to-all(bf16[8,144,256]{2,1,0:T(8,128)(2,1)S(1)} %shard_map.57), channel_id=1, replica_groups=mesh['zh'=2,'zl'=4,'y'=8,'x'=4,'c'=2] {'x','c'}, dimensions={0} | all-to-all | bytes 1179648 | tf_op jit(solution)/shard_map/all_to_all | solution.py:180
  127.9 0.8 shard_map.58
  128.7 3.9 %all-to-all-start.6 = ((bf16[32,16,128]{2,1,0:T(8,128)(2,1)}), bf16[32,16,128]{2,1,0:T(8,128)(2,1)S(1)}, u32[]{:S(2)}, u32[]{:S(2)}) async-start(bf16[32,16,128]{2,1,0:T(8,128)(2,1)} %shard_map.58), calls=%async_computation.6 | async-start | bytes 262144 | tf_op jit(solution)/shard_map/all_to_all | solution.py:180
  133.2 9.3 %all-to-all-done.6.in_ref = bf16[32,16,128]{2,1,0:T(8,128)(2,1)S(1)} async-done(((bf16[32,16,128]{2,1,0:T(8,128)(2,1)}), bf16[32,16,128]{2,1,0:T(8,128)(2,1)S(1)}, u32[]{:S(2)}, u32[]{:S(2)}) %all-to-all-start.6) | async-done | bytes 131104 | tf_op jit(solution)/shard_map/all_to_all | solution.py:180
  142.6 0.8 shard_map.59
Async XLA Ops:
  0.0 44.9 %copy-start = (bf16[1536,128]{1,0:T(8,128)(2,1)S(1)}, bf16[1536,128]{1,0:T(8,128)(2,1)}, u32[]{:S(2)}) copy-start(bf16[1536,128]{1,0:T(8,128)(2,1)} %param.7) | copy-start | bytes 1179652
  45.9 23.7 %all-to-all-start.4 = ((bf16[8,384,128]{2,1,0:T(8,128)(2,1)}), bf16[8,384,128]{2,1,0:T(8,128)(2,1)}, u32[]{:S(2)}, u32[]{:S(2)}) async-start(bf16[8,384,128]{2,1,0:T(8,128)(2,1)} %bitcast.4), calls=%async_computation.4 | async-start | bytes 1572864 | tf_op jit(solution)/shard_map/all_to_all | solution.py:180
  50.1 8.6 %collective-permute-start = (bf16[4,512,128]{2,1,0:T(8,128)(2,1)S(1)}, bf16[4,512,128]{2,1,0:T(8,128)(2,1)S(1)}, u32[]{:S(2)}, u32[]{:S(2)}) collective-permute-start(bf16[4,512,128]{2,1,0:T(8,128)(2,1)S(1)} %all_to_all.37.own_ref), channel_id=1, source_target_pairs={{0,1},{1,0},{2,3},{3,2},{4,5},{5,4},{6,7},{7,6},{8,9},{9,8},{10,11... | collective-permute-start | bytes 1572872 | tf_op jit(solution)/shard_map/ppermute | solution.py:188
  128.7 13.9 %all-to-all-start.6 = ((bf16[32,16,128]{2,1,0:T(8,128)(2,1)}), bf16[32,16,128]{2,1,0:T(8,128)(2,1)S(1)}, u32[]{:S(2)}, u32[]{:S(2)}) async-start(bf16[32,16,128]{2,1,0:T(8,128)(2,1)} %shard_map.58), calls=%async_computation.6 | async-start | bytes 262144 | tf_op jit(solution)/shard_map/all_to_all | solution.py:180

commit v3 on v2

v3 whole, which is shorter than its diff:
```python
import jax
import jax.numpy as jnp
from jax import lax
from jax.experimental import pallas as pl
from jax.experimental.pallas import tpu as pltpu
from jax.sharding import Mesh, PartitionSpec as P


F32 = jnp.float32
BF16 = jnp.bfloat16
ALL = ("z", "y", "x", "c")
VMEM = pl.BlockSpec(memory_space=pltpu.VMEM)
SMEM = pl.BlockSpec(memory_space=pltpu.SMEM)
OUTER = pl.BlockSpec(memory_space=pltpu.VMEM)
STAY = pl.BlockSpec(memory_space=pl.ANY)


def call(kernel, out_shape, in_specs, *args, scratch=(), out_memory=pltpu.VMEM):
    args = [
        pltpu.with_memory_space_constraint(a, pltpu.VMEM) if spec is VMEM else a
        for a, spec in zip(args, in_specs)
    ]
    return pl.pallas_call(
        kernel,
        out_shape=out_memory(*out_shape) if out_memory else jax.ShapeDtypeStruct(*out_shape),
        in_specs=in_specs,
        out_specs=VMEM,
        scratch_shapes=list(scratch),
    )(*args)


def split(v):
    high = v.astype(BF16)
    return high, (v - high.astype(F32)).astype(BF16)


def iota(shape, axis):
    return lax.broadcasted_iota(jnp.int32, shape, axis)


def select_kernel(index_ref, hidden_ref, out_ref):
    chosen = jnp.where(iota((256, 64), 0) == index_ref[...], 1.0, 0.0).astype(BF16)
    picked = lax.dot_general(
        chosen, hidden_ref[...], (((0,), (0,)), ((), ())), preferred_element_type=F32
    ).astype(BF16)
    for i in range(8):
        out_ref[i] = picked


def logits_kernel(core_ref, own_ref, other_ref, head_ref, out_ref, held_ref, sems):
    copies = [
        pltpu.make_async_copy(head_ref.at[:, pl.ds(n * 256, 256)], held_ref.at[n], sems.at[n]) for n in range(6)
    ]
    for copy in copies:
        copy.start()
    first = core_ref[0] == 0
    features = []
    for x in range(4):
        own, other = own_ref[x], other_ref[x]
        features.append(jnp.where(first, own, other))
        features.append(jnp.where(first, other, own))
    lhs = jnp.concatenate(features, axis=1)
    for n in range(6):
        copies[n].wait()
        part = jnp.dot(lhs, held_ref[n], preferred_element_type=F32).astype(BF16)
        for owner in range(8):
            out_ref[owner, :, pl.ds(n * 256, 256)] = part[owner * 64 : owner * 64 + 64]


def project_kernel(parts_ref, basis_ref, out_ref, held_ref, sems):
    copies = [
        pltpu.make_async_copy(basis_ref.at[pl.ds(2 * j, 2)], held_ref.at[j], sems.at[j]) for j in range(4)
    ]
    for copy in copies:
        copy.start()
    logits = parts_ref[0].astype(F32)
    for i in range(1, 8):
        logits = logits + parts_ref[i].astype(F32)
    top_high, top_low = split(jnp.max(logits, axis=1, keepdims=True))
    top_high, top_low = top_high.astype(F32), top_low.astype(F32)
    weights = jnp.exp(logits - (top_high + top_low))
    den_high, den_low = split(jnp.sum(weights, axis=1, keepdims=True))
    wei_high, wei_low = split(jnp.sum(weights * logits, axis=1, keepdims=True))
    lane = iota((64, 128), 1)
    stats = jnp.zeros((64, 128), F32)
    for i, v in enumerate([top_high, top_low, den_high, den_low, wei_high, wei_low]):
        stats = jnp.where(lane == i, v.astype(F32), stats)
    stats = jnp.concatenate([jnp.zeros((64, 128), F32), stats], axis=0).T[0:16, :]
    high, low = split(logits)
    lhs = jnp.concatenate([high, low, jnp.ones((128, 1536), BF16)], axis=0)
    row, lane = iota((16, 128), 0), iota((16, 128), 1)
    for j in range(4):
        copies[j].wait()
        rhs = jnp.concatenate([held_ref[j, 0], held_ref[j, 1]], axis=1)
        both = jnp.dot(lhs, rhs, preferred_element_type=F32)
        turned = jnp.concatenate([both[0:64] + both[64:128], jnp.zeros((64, 256), F32)], axis=0).T
        for half in range(2):
            sums_high, sums_low = split(both[128:136, half * 128 : half * 128 + 128])
            sums_high, sums_low = sums_high.astype(F32), sums_low.astype(F32)
            for block in range(8):
                start = half * 128 + block * 16
                shift = (64 - 16 * block) % 128
                line_high = pltpu.roll(sums_high, shift, 1)[0:1]
                line_low = pltpu.roll(sums_low, shift, 1)[0:1]
                extra = jnp.where(row == 6, line_high, jnp.where(row == 7, line_low, stats))
                tile = jnp.where(lane < 64, turned[start : start + 16], extra)
                out_ref[16 * j + 8 * half + block] = tile.astype(BF16)


def merge(tiles):
    tops = [t[0:1] + t[1:2] for t in tiles]
    top = tops[0]
    for t in tops[1:]:
        top = jnp.maximum(top, t)
    denominator, weighted, sums = 0.0, 0.0, 0.0
    for mine, tile in zip(tops, tiles):
        scale = jnp.exp(mine - top)
        denominator = denominator + scale * (tile[2:3] + tile[3:4])
        weighted = weighted + scale * (tile[4:5] + tile[5:6])
        sums = sums + (tile[6:7] + tile[7:8])
    return top, denominator, weighted, sums


def finish_kernel(count_ref, in_ref, out_ref):
    tiles = [in_ref[i].astype(F32) for i in range(64)]
    total = tiles[0]
    for t in tiles[1:]:
        total = total + t
    _, denominator, weighted, sums = merge(tiles)
    expected = pltpu.roll(jnp.broadcast_to(weighted / denominator, (8, 128)), 64, 1)[0:1]
    row, lane = iota((16, 128), 0), iota((16, 128), 1)
    column = jnp.sum(jnp.where(lane == row + 64, sums, 0.0), axis=1, keepdims=True)
    result = jnp.where(lane < count_ref[0], total - expected * column, 0.0)
    out_ref[...] = result[:, 0:64]


def shards(hidden, head_weight, vocab_basis, keep_index, counts):
    def exchange(v, axes):
        return lax.all_to_all(v, axes, 0, 0, tiled=True)

    core = lax.axis_index("c").astype(jnp.int32).reshape(1)
    basis = lax.all_gather(vocab_basis, "z")
    owned = call(select_kernel, ((8, 64, 128), BF16), [OUTER, OUTER], keep_index.reshape(1, 64), hidden)
    sliced = exchange(exchange(owned, "y"), "z")
    mine = exchange(jnp.broadcast_to(sliced.reshape(1, 512, 128), (4, 512, 128)), "x")
    theirs = lax.ppermute(mine, "c", [(0, 1), (1, 0)])
    parts = call(
        logits_kernel,
        ((8, 64, 1536), BF16),
        [SMEM, VMEM, VMEM, STAY],
        core,
        mine,
        theirs,
        head_weight,
        scratch=[pltpu.VMEM((6, 1024, 256), BF16), pltpu.SemaphoreType.DMA((6,))],
    )
    tiles = call(
        project_kernel,
        ((64, 16, 128), BF16),
        [VMEM, STAY],
        exchange(parts, "z"),
        basis,
        scratch=[pltpu.VMEM((4, 2, 1536, 128), BF16), pltpu.SemaphoreType.DMA((4,))],
    )
    tiles = exchange(tiles, ("y", "x", "c"))
    return call(finish_kernel, ((16, 64), F32), [SMEM, VMEM], counts, tiles, out_memory=None).T


def solution(mesh):
    grid = Mesh(mesh.devices.reshape(8, 8, 4, 2), ALL)
    rows, cols = "z", ("y", "x", "c")
    in_specs = (P(rows, cols), P(rows, cols), P(cols, rows), P(rows), P(rows))
    return jax.shard_map(shards, mesh=grid, in_specs=in_specs, out_specs=P(rows, cols), check_vma=False)
```

time: 144 us -> 140 us (0.972)
  between operations: 0.71 us -> 14.1 us
  blocking collectives: 99.7 us -> 88.1 us
  starting transfers between devices: 15.1 us -> 11.6 us
  waiting for transfers between devices: 18.1 us -> 14.7 us
  Pallas kernels: 8.63 us -> 11.5 us
    all_to_all x5 -> x4, blocking collectives: 99.7 us -> 88.1 us  [exchange(): return lax.all_to_all(v, axes, 0, 0, tiled=True)]
    all_to_all x2 -> x1, waiting for transfers between devices: 16.6 us -> 12.5 us  [exchange(): return lax.all_to_all(v, axes, 0, 0, tiled=True)]
    all_to_all x2 -> x1, starting transfers between devices: 8.06 us -> 4.57 us  [exchange(): return lax.all_to_all(v, axes, 0, 0, tiled=True)]
    pallas_call x5 -> x4, Pallas kernels: 8.63 us -> 11.5 us  [call(): pl.pallas_call(kernel, out_shape=out_memory(*out_shape) if out_memory els...]
  transfers between devices with their start and end apart: 3 -> 3, of which waited for: 3 -> 2; matrix products, arithmetic and copies ran while one was open for 0% -> 0% of each run, Pallas kernels for 3% -> 4%
where the time goes in v3:
time: 140 us
  blocking collectives  88.1 us (63%)
  waiting for transfers between devices  14.7 us (10%)
  between operations  14.1 us (10%)
  starting transfers between devices  11.6 us (8%)
  Pallas kernels  11.5 us (8%)
    all_to_all x4, blocking collectives, exchange(): return lax.all_to_all(v, axes, 0, 0, tiled=True)  88.1 us
    all_to_all x1, waiting for transfers between devices, exchange(): return lax.all_to_all(v, axes, 0, 0, tiled=True)  12.5 us
    pallas_call x4, Pallas kernels, call(): pl.pallas_call(kernel, out_shape=out_memory(*out_shape) if out_memory els...  11.5 us
    ppermute x1, starting transfers between devices, shards(): theirs = lax.ppermute(mine, 'c', [(0, 1), (1, 0)])  6.99 us
    all_to_all x1, starting transfers between devices, exchange(): return lax.all_to_all(v, axes, 0, 0, tiled=True)  4.57 us
  transfers between devices with their start and end apart: 3, of which 2 were waited for; matrix products, arithmetic and copies ran while one was open for 0% of the time, Pallas kernels for 4%

profile of v3, /device:TPU:1, one launch (start us, length us, event | category | flops | bytes accessed | tf_op | source)
XLA Modules:
  0.0 140.1 jit_solution(17313246205974042589)
XLA Ops:
  6.5 0.0 all-gather.3.cloned.1.call-start
  6.5 0.7 all-gather.3.cloned.1.call-update
  7.3 1.0 shard_map.55
  8.3 15.4 %all_to_all.25 = bf16[8,64,128]{2,1,0:T(8,128)(2,1)S(1)} all-to-all(bf16[8,64,128]{2,1,0:T(8,128)(2,1)S(1)} %shard_map.55), channel_id=1, replica_groups=mesh['z'=8,'y'=8,'x'=4,'c'=2] {'y'}, dimensions={0} | all-to-all | bytes 262144 | tf_op jit(solution)/shard_map/all_to_all | solution.py:139
  23.7 19.1 %all_to_all.26 = bf16[8,64,128]{2,1,0:T(8,128)(2,1)S(1)} all-to-all(bf16[8,64,128]{2,1,0:T(8,128)(2,1)S(1)} %all_to_all.25), channel_id=1, replica_groups=mesh['z'=8,'y'=8,'x'=4,'c'=2] {'z'}, dimensions={0} | all-to-all | bytes 262144 | tf_op jit(solution)/shard_map/all_to_all | solution.py:139
  42.8 0.1 broadcast_in_dim.8
  42.9 10.8 %all_to_all.27.own_ref = bf16[4,512,128]{2,1,0:T(8,128)(2,1)S(1)} all-to-all(bf16[4,512,128]{2,1,0:T(8,128)(2,1)S(1)} %broadcast_in_dim.8), channel_id=1, replica_groups=mesh['z'=8,'y'=8,'x'=4,'c'=2] {'x'}, dimensions={0} | all-to-all | bytes 1048576 | tf_op jit(solution)/shard_map/all_to_all | solution.py:139
  53.7 7.0 %collective-permute-start = (bf16[4,512,128]{2,1,0:T(8,128)(2,1)S(1)}, bf16[4,512,128]{2,1,0:T(8,128)(2,1)S(1)}, u32[]{:S(2)}, u32[]{:S(2)}) collective-permute-start(bf16[4,512,128]{2,1,0:T(8,128)(2,1)S(1)} %all_to_all.27.own_ref), channel_id=1, source_target_pairs={{0,1},{1,0},{2,3},{3,2},{4,5},{5,4},{6,7},{7,6},{8,9},{9,8},{10,11... | collective-permute-start | bytes 1572872 | tf_op jit(solution)/shard_map/ppermute | solution.py:146
  60.7 1.5 %collective-permute-done.other_ref = bf16[4,512,128]{2,1,0:T(8,128)(2,1)S(1)} collective-permute-done((bf16[4,512,128]{2,1,0:T(8,128)(2,1)S(1)}, bf16[4,512,128]{2,1,0:T(8,128)(2,1)S(1)}, u32[]{:S(2)}, u32[]{:S(2)}) %collective-permute-start) | collective-permute-done | bytes 524320 | tf_op jit(solution)/shard_map/ppermute | solution.py:146
  62.2 5.2 %shard_map.56 = bf16[8,64,1536]{2,1,0:T(8,128)(2,1)S(1)} custom-call(s32[1]{0:T(128)} %bitcast.core_ref, bf16[4,512,128]{2,1,0:T(8,128)(2,1)S(1)} %all_to_all.27.own_ref, bf16[4,512,128]{2,1,0:T(8,128)(2,1)S(1)} %collective-permute-done.other_ref, bf16[1024,1536]{1,0:T(8,128)(2,1)} %head_ref.1), custom_call_target="tpu_custom_call" | custom-call | tf_op jit(solution)/shard_map/pallas_call | solution.py:23
  67.4 42.8 %all_to_all.28.parts_ref = bf16[8,64,1536]{2,1,0:T(8,128)(2,1)S(1)} all-to-all(bf16[8,64,1536]{2,1,0:T(8,128)(2,1)S(1)} %shard_map.56), channel_id=1, replica_groups=mesh['z'=8,'y'=8,'x'=4,'c'=2] {'z'}, dimensions={0} | all-to-all | bytes 3145728 | tf_op jit(solution)/shard_map/all_to_all | solution.py:139
  110.3 0.0 all-gather.3.cloned.1.call-done
  110.3 4.4 %shard_map.57 = bf16[64,16,128]{2,1,0:T(8,128)(2,1)} custom-call(bf16[8,64,1536]{2,1,0:T(8,128)(2,1)S(1)} %all_to_all.28.parts_ref, bf16[8,1536,128]{2,1,0:T(8,128)(2,1)} %bitcast.5), custom_call_target="tpu_custom_call" | custom-call | tf_op jit(solution)/shard_map/pallas_call | solution.py:23
  114.7 4.6 %all-to-all-start.4 = ((bf16[64,16,128]{2,1,0:T(8,128)(2,1)}), bf16[64,16,128]{2,1,0:T(8,128)(2,1)S(1)}, u32[]{:S(2)}, u32[]{:S(2)}) async-start(bf16[64,16,128]{2,1,0:T(8,128)(2,1)} %shard_map.57), calls=%async_computation.4 | async-start | bytes 524288 | tf_op jit(solution)/shard_map/all_to_all | solution.py:139
  119.9 12.5 %all-to-all-done.4.in_ref = bf16[64,16,128]{2,1,0:T(8,128)(2,1)S(1)} async-done(((bf16[64,16,128]{2,1,0:T(8,128)(2,1)}), bf16[64,16,128]{2,1,0:T(8,128)(2,1)S(1)}, u32[]{:S(2)}, u32[]{:S(2)}) %all-to-all-start.4) | async-done | bytes 262176 | tf_op jit(solution)/shard_map/all_to_all | solution.py:139
  132.4 0.8 shard_map.58
Async XLA Ops:
  6.5 103.7 %all-gather.3.cloned.1.call-start = ((), (), s32[]{:S(2)}) async-start(), calls=%async_computation.5 | async-start | bytes 3538944 | tf_op jit(solution)/shard_map/all_gather | solution.py:142
  53.7 8.5 %collective-permute-start = (bf16[4,512,128]{2,1,0:T(8,128)(2,1)S(1)}, bf16[4,512,128]{2,1,0:T(8,128)(2,1)S(1)}, u32[]{:S(2)}, u32[]{:S(2)}) collective-permute-start(bf16[4,512,128]{2,1,0:T(8,128)(2,1)S(1)} %all_to_all.27.own_ref), channel_id=1, source_target_pairs={{0,1},{1,0},{2,3},{3,2},{4,5},{5,4},{6,7},{7,6},{8,9},{9,8},{10,11... | collective-permute-start | bytes 1572872 | tf_op jit(solution)/shard_map/ppermute | solution.py:146
  114.7 17.7 %all-to-all-start.4 = ((bf16[64,16,128]{2,1,0:T(8,128)(2,1)}), bf16[64,16,128]{2,1,0:T(8,128)(2,1)S(1)}, u32[]{:S(2)}, u32[]{:S(2)}) async-start(bf16[64,16,128]{2,1,0:T(8,128)(2,1)} %shard_map.57), calls=%async_computation.4 | async-start | bytes 524288 | tf_op jit(solution)/shard_map/all_to_all | solution.py:139
Sparse Core Ops, SparseCore 0:
  9.4 56.4 all-gather.2

commit v4 on v3

--- a/solution.py
+++ b/solution.py
@@ -40,11 +40,9 @@
 
 def select_kernel(index_ref, hidden_ref, out_ref):
     chosen = jnp.where(iota((256, 64), 0) == index_ref[...], 1.0, 0.0).astype(BF16)
-    picked = lax.dot_general(
+    out_ref[...] = lax.dot_general(
         chosen, hidden_ref[...], (((0,), (0,)), ((), ())), preferred_element_type=F32
     ).astype(BF16)
-    for i in range(8):
-        out_ref[i] = picked
 
 
 def logits_kernel(core_ref, own_ref, other_ref, head_ref, out_ref, held_ref, sems):
@@ -54,17 +52,23 @@
     for copy in copies:
         copy.start()
     first = core_ref[0] == 0
-    features = []
-    for x in range(4):
-        own, other = own_ref[x], other_ref[x]
-        features.append(jnp.where(first, own, other))
-        features.append(jnp.where(first, other, own))
-    lhs = jnp.concatenate(features, axis=1)
+    lhs = []
+    for group in range(2):
+        rows = pl.ds(group * 256, 256)
+        features = []
+        for x in range(4):
+            picks = [16 * group + 4 * o + x for o in range(4)]
+            own = jnp.concatenate([own_ref[p] for p in picks], axis=0)
+            other = jnp.concatenate([other_ref[p] for p in picks], axis=0)
+            features.append(jnp.where(first, own, other))
+            features.append(jnp.where(first, other, own))
+        lhs.append(jnp.concatenate(features, axis=1))
     for n in range(6):
         copies[n].wait()
-        part = jnp.dot(lhs, held_ref[n], preferred_element_type=F32).astype(BF16)
-        for owner in range(8):
-            out_ref[owner, :, pl.ds(n * 256, 256)] = part[owner * 64 : owner * 64 + 64]
+        for group in range(2):
+            part = jnp.dot(lhs[group], held_ref[n], preferred_element_type=F32).astype(BF16)
+            for owner in range(4):
+                out_ref[group * 4 + owner, :, pl.ds(n * 256, 256)] = part[owner * 64 : owner * 64 + 64]
 
 
 def project_kernel(parts_ref, basis_ref, out_ref, held_ref, sems):
@@ -87,7 +91,7 @@
         stats = jnp.where(lane == i, v.astype(F32), stats)
     stats = jnp.concatenate([jnp.zeros((64, 128), F32), stats], axis=0).T[0:16, :]
     high, low = split(logits)
-    lhs = jnp.concatenate([high, low, jnp.ones((128, 1536), BF16)], axis=0)
+    lhs = jnp.concatenate([high, low, jnp.ones((16, 1536), BF16)], axis=0)
     row, lane = iota((16, 128), 0), iota((16, 128), 1)
     for j in range(4):
         copies[j].wait()
@@ -140,9 +144,10 @@
 
     core = lax.axis_index("c").astype(jnp.int32).reshape(1)
     basis = lax.all_gather(vocab_basis, "z")
-    owned = call(select_kernel, ((8, 64, 128), BF16), [OUTER, OUTER], keep_index.reshape(1, 64), hidden)
-    sliced = exchange(exchange(owned, "y"), "z")
-    mine = exchange(jnp.broadcast_to(sliced.reshape(1, 512, 128), (4, 512, 128)), "x")
+    owned = call(select_kernel, ((64, 128), BF16), [OUTER, OUTER], keep_index.reshape(1, 64), hidden)
+    pairs = [((z * 8 + y) * 8 + k, (y * 8 + z) * 8 + k) for z in range(8) for y in range(8) for k in range(8)]
+    moved = lax.ppermute(owned, ("z", "y", "x", "c"), pairs)
+    mine = exchange(jnp.broadcast_to(moved[None], (32, 64, 128)), ("y", "x"))
     theirs = lax.ppermute(mine, "c", [(0, 1), (1, 0)])
     parts = call(
         logits_kernel,

time: 140 us -> 136 us (0.971)
  blocking collectives: 88.1 us -> 84.5 us
  Pallas kernels: 11.5 us -> 9.43 us
    all_to_all x4 -> x2, blocking collectives: 88.1 us -> 84.5 us  [exchange(): return lax.all_to_all(v, axes, 0, 0, tiled=True)]
    pallas_call x4, Pallas kernels: 11.5 us -> 9.43 us  [call(): pl.pallas_call(kernel, out_shape=out_memory(*out_shape) if out_memory els...]
    all_to_all x1, starting transfers between devices: 4.57 us -> 6.47 us  [exchange(): return lax.all_to_all(v, axes, 0, 0, tiled=True)]
  transfers between devices with their start and end apart: 3 -> 4, of which waited for: 2 -> 2; matrix products, arithmetic and copies ran while one was open for 0% -> 0% of each run, Pallas kernels for 4% -> 4%
where the time goes in v4:
time: 136 us
  blocking collectives  84.5 us (62%)
  waiting for transfers between devices  14.7 us (11%)
  between operations  14.1 us (10%)
  starting transfers between devices  12.9 us (9%)
  Pallas kernels  9.43 us (7%)
    all_to_all x2, blocking collectives, exchange(): return lax.all_to_all(v, axes, 0, 0, tiled=True)  84.5 us
    all_to_all x1, waiting for transfers between devices, exchange(): return lax.all_to_all(v, axes, 0, 0, tiled=True)  12.4 us
    pallas_call x4, Pallas kernels, call(): pl.pallas_call(kernel, out_shape=out_memory(*out_shape) if out_memory els...  9.43 us
    all_to_all x1, starting transfers between devices, exchange(): return lax.all_to_all(v, axes, 0, 0, tiled=True)  6.47 us
    ppermute x1, starting transfers between devices, shards(): theirs = lax.ppermute(mine, 'c', [(0, 1), (1, 0)])  5.75 us
  transfers between devices with their start and end apart: 4, of which 2 were waited for; matrix products, arithmetic and copies ran while one was open for 0% of the time, Pallas kernels for 4%

profile of v4, /device:TPU:1, one launch (start us, length us, event | category | flops | bytes accessed | tf_op | source)
XLA Modules:
  0.0 135.7 jit_solution(80136238111939410)
XLA Ops:
  6.5 0.0 all-gather.3.cloned.1.call-start
  6.5 0.7 all-gather.3.cloned.1.call-update
  7.3 1.0 shard_map.55
  8.3 0.7 collective-permute-start
  9.0 0.0 collective-permute-done
  9.0 0.1 broadcast_in_dim.2
  9.1 37.8 %all_to_all.15.own_ref = bf16[32,64,128]{2,1,0:T(8,128)(2,1)S(1)} all-to-all(bf16[32,64,128]{2,1,0:T(8,128)(2,1)S(1)} %broadcast_in_dim.2), channel_id=1, replica_groups=mesh['z'=8,'y'=8,'x'=4,'c'=2] {'y','x'}, dimensions={0} | all-to-all | bytes 1048576 | tf_op jit(solution)/shard_map/all_to_all | solution.py:143
  46.9 5.8 %collective-permute-start.1 = (bf16[32,64,128]{2,1,0:T(8,128)(2,1)S(1)}, bf16[32,64,128]{2,1,0:T(8,128)(2,1)S(1)}, u32[]{:S(2)}, u32[]{:S(2)}) collective-permute-start(bf16[32,64,128]{2,1,0:T(8,128)(2,1)S(1)} %all_to_all.15.own_ref), channel_id=1, source_target_pairs={{0,1},{1,0},{2,3},{3,2},{4,5},{5,4},{6,7},{7,6},{8,9},{9,8},{10,11... | collective-permute-start | bytes 1572872 | tf_op jit(solution)/shard_map/ppermute | solution.py:151
  52.7 1.5 %collective-permute-done.1.other_ref = bf16[32,64,128]{2,1,0:T(8,128)(2,1)S(1)} collective-permute-done((bf16[32,64,128]{2,1,0:T(8,128)(2,1)S(1)}, bf16[32,64,128]{2,1,0:T(8,128)(2,1)S(1)}, u32[]{:S(2)}, u32[]{:S(2)}) %collective-permute-start.1) | collective-permute-done | bytes 524320 | tf_op jit(solution)/shard_map/ppermute | solution.py:151
  54.2 3.7 %shard_map.56 = bf16[8,64,1536]{2,1,0:T(8,128)(2,1)S(1)} custom-call(s32[1]{0:T(128)} %bitcast.core_ref, bf16[32,64,128]{2,1,0:T(8,128)(2,1)S(1)} %all_to_all.15.own_ref, bf16[32,64,128]{2,1,0:T(8,128)(2,1)S(1)} %collective-permute-done.1.other_ref, bf16[1024,1536]{1,0:T(8,128)(2,1)} %head_ref.1), custom_call_target="tpu_custom_call" | custom-call | tf_op jit(solution)/shard_map/pallas_call | solution.py:23
  57.9 46.7 %all_to_all.16.parts_ref = bf16[8,64,1536]{2,1,0:T(8,128)(2,1)S(1)} all-to-all(bf16[8,64,1536]{2,1,0:T(8,128)(2,1)S(1)} %shard_map.56), channel_id=1, replica_groups=mesh['z'=8,'y'=8,'x'=4,'c'=2] {'z'}, dimensions={0} | all-to-all | bytes 3145728 | tf_op jit(solution)/shard_map/all_to_all | solution.py:143
  104.6 0.0 all-gather.3.cloned.1.call-done
  104.7 3.8 %shard_map.57 = bf16[64,16,128]{2,1,0:T(8,128)(2,1)} custom-call(bf16[8,64,1536]{2,1,0:T(8,128)(2,1)S(1)} %all_to_all.16.parts_ref, bf16[8,1536,128]{2,1,0:T(8,128)(2,1)} %bitcast.4), custom_call_target="tpu_custom_call" | custom-call | tf_op jit(solution)/shard_map/pallas_call | solution.py:23
  108.5 6.5 %all-to-all-start.2 = ((bf16[64,16,128]{2,1,0:T(8,128)(2,1)}), bf16[64,16,128]{2,1,0:T(8,128)(2,1)S(1)}, u32[]{:S(2)}, u32[]{:S(2)}) async-start(bf16[64,16,128]{2,1,0:T(8,128)(2,1)} %shard_map.57), calls=%async_computation.2 | async-start | bytes 524288 | tf_op jit(solution)/shard_map/all_to_all | solution.py:143
  115.6 12.4 %all-to-all-done.2.in_ref = bf16[64,16,128]{2,1,0:T(8,128)(2,1)S(1)} async-done(((bf16[64,16,128]{2,1,0:T(8,128)(2,1)}), bf16[64,16,128]{2,1,0:T(8,128)(2,1)S(1)}, u32[]{:S(2)}, u32[]{:S(2)}) %all-to-all-start.2) | async-done | bytes 262176 | tf_op jit(solution)/shard_map/all_to_all | solution.py:143
  128.1 0.8 shard_map.58
Async XLA Ops:
  6.5 98.1 %all-gather.3.cloned.1.call-start = ((), (), s32[]{:S(2)}) async-start(), calls=%async_computation.3 | async-start | bytes 3538944 | tf_op jit(solution)/shard_map/all_gather | solution.py:146
  8.3 0.7 collective-permute-start
  46.9 7.3 %collective-permute-start.1 = (bf16[32,64,128]{2,1,0:T(8,128)(2,1)S(1)}, bf16[32,64,128]{2,1,0:T(8,128)(2,1)S(1)}, u32[]{:S(2)}, u32[]{:S(2)}) collective-permute-start(bf16[32,64,128]{2,1,0:T(8,128)(2,1)S(1)} %all_to_all.15.own_ref), channel_id=1, source_target_pairs={{0,1},{1,0},{2,3},{3,2},{4,5},{5,4},{6,7},{7,6},{8,9},{9,8},{10,11... | collective-permute-start | bytes 1572872 | tf_op jit(solution)/shard_map/ppermute | solution.py:151
  108.5 19.6 %all-to-all-start.2 = ((bf16[64,16,128]{2,1,0:T(8,128)(2,1)}), bf16[64,16,128]{2,1,0:T(8,128)(2,1)S(1)}, u32[]{:S(2)}, u32[]{:S(2)}) async-start(bf16[64,16,128]{2,1,0:T(8,128)(2,1)} %shard_map.57), calls=%async_computation.2 | async-start | bytes 524288 | tf_op jit(solution)/shard_map/all_to_all | solution.py:143
Sparse Core Ops, SparseCore 0:
  9.4 53.6 all-gather.2

commit v5 on v4

--- a/solution.py
+++ b/solution.py
@@ -20,11 +20,15 @@
         pltpu.with_memory_space_constraint(a, pltpu.VMEM) if spec is VMEM else a
         for a, spec in zip(args, in_specs)
     ]
+    if isinstance(out_shape, list):
+        shapes = [pltpu.VMEM(*o) for o in out_shape]
+    else:
+        shapes = out_memory(*out_shape) if out_memory else jax.ShapeDtypeStruct(*out_shape)
     return pl.pallas_call(
         kernel,
-        out_shape=out_memory(*out_shape) if out_memory else jax.ShapeDtypeStruct(*out_shape),
+        out_shape=shapes,
         in_specs=in_specs,
-        out_specs=VMEM,
+        out_specs=[VMEM] * len(out_shape) if isinstance(out_shape, list) else VMEM,
         scratch_shapes=list(scratch),
     )(*args)
 
@@ -71,7 +75,7 @@
                 out_ref[group * 4 + owner, :, pl.ds(n * 256, 256)] = part[owner * 64 : owner * 64 + 64]
 
 
-def project_kernel(parts_ref, basis_ref, out_ref, held_ref, sems):
+def project_kernel(core_ref, parts_ref, basis_ref, keep_ref, send_ref, held_ref, tiles_ref, sems):
     copies = [
         pltpu.make_async_copy(basis_ref.at[pl.ds(2 * j, 2)], held_ref.at[j], sems.at[j]) for j in range(4)
     ]
@@ -108,7 +112,9 @@
                 line_low = pltpu.roll(sums_low, shift, 1)[0:1]
                 extra = jnp.where(row == 6, line_high, jnp.where(row == 7, line_low, stats))
                 tile = jnp.where(lane < 64, turned[start : start + 16], extra)
-                out_ref[16 * j + 8 * half + block] = tile.astype(BF16)
+                tiles_ref[block % 2, 8 * j + 4 * half + block // 2] = tile.astype(BF16)
+    keep_ref[...] = tiles_ref[core_ref[0]]
+    send_ref[...] = tiles_ref[1 - core_ref[0]]
 
 
 def merge(tiles):
@@ -125,8 +131,23 @@
     return top, denominator, weighted, sums
 
 
+def pair_kernel(keep_ref, recv_ref, out_ref):
+    top, denominator, weighted, _ = merge([keep_ref[0].astype(F32), recv_ref[0].astype(F32)])
+    row, lane = iota((16, 128), 0), iota((16, 128), 1)
+    stats = jnp.zeros((16, 128), F32)
+    for i, v in enumerate([h for v in (top, denominator, weighted) for h in split(v)]):
+        stats = jnp.where(row == i, v.astype(F32), stats)
+    shared = jnp.logical_and(lane >= 64, row < 6)
+    for i in range(32):
+        keep, recv = keep_ref[i].astype(F32), recv_ref[i].astype(F32)
+        sums_high, sums_low = split((keep[6:7] + keep[7:8]) + (recv[6:7] + recv[7:8]))
+        tile = jnp.where(row == 6, sums_high.astype(F32), sums_low.astype(F32))
+        tile = jnp.where(jnp.logical_and(lane >= 64, row < 8), tile, keep + recv)
+        out_ref[i] = jnp.where(shared, stats, tile).astype(BF16)
+
+
 def finish_kernel(count_ref, in_ref, out_ref):
-    tiles = [in_ref[i].astype(F32) for i in range(64)]
+    tiles = [in_ref[i].astype(F32) for i in range(32)]
     total = tiles[0]
     for t in tiles[1:]:
         total = total + t
@@ -143,8 +164,9 @@
         return lax.all_to_all(v, axes, 0, 0, tiled=True)
 
     core = lax.axis_index("c").astype(jnp.int32).reshape(1)
-    basis = lax.all_gather(vocab_basis, "z")
     owned = call(select_kernel, ((64, 128), BF16), [OUTER, OUTER], keep_index.reshape(1, 64), hidden)
+    late_basis, owned = lax.optimization_barrier((vocab_basis, owned))
+    basis = lax.all_gather(late_basis, "z")
     pairs = [((z * 8 + y) * 8 + k, (y * 8 + z) * 8 + k) for z in range(8) for y in range(8) for k in range(8)]
     moved = lax.ppermute(owned, ("z", "y", "x", "c"), pairs)
     mine = exchange(jnp.broadcast_to(moved[None], (32, 64, 128)), ("y", "x"))
@@ -159,15 +181,21 @@
         head_weight,
         scratch=[pltpu.VMEM((6, 1024, 256), BF16), pltpu.SemaphoreType.DMA((6,))],
     )
-    tiles = call(
+    keep, send = call(
         project_kernel,
-        ((64, 16, 128), BF16),
-        [VMEM, STAY],
+        [((32, 16, 128), BF16), ((32, 16, 128), BF16)],
+        [SMEM, VMEM, STAY],
+        core,
         exchange(parts, "z"),
         basis,
-        scratch=[pltpu.VMEM((4, 2, 1536, 128), BF16), pltpu.SemaphoreType.DMA((4,))],
+        scratch=[
+            pltpu.VMEM((4, 2, 1536, 128), BF16),
+            pltpu.VMEM((2, 32, 16, 128), BF16),
+            pltpu.SemaphoreType.DMA((4,)),
+        ],
     )
-    tiles = exchange(tiles, ("y", "x", "c"))
+    tiles = call(pair_kernel, ((32, 16, 128), BF16), [VMEM, VMEM], keep, lax.ppermute(send, "c", [(0, 1), (1, 0)]))
+    tiles = exchange(tiles, ("y", "x"))
     return call(finish_kernel, ((16, 64), F32), [SMEM, VMEM], counts, tiles, out_memory=None).T
 
 

time: 136 us -> 134 us (0.985)
  waiting for transfers between devices: 14.7 us -> 11.2 us
  starting transfers between devices: 12.9 us -> 14.3 us
    all_to_all x1, waiting for transfers between devices: 12.4 us -> 8.7 us  [exchange(): return lax.all_to_all(v, axes, 0, 0, tiled=True)]
    ppermute x0 -> x1, starting transfers between devices: none -> 3.61 us  [shards(): lax.ppermute(send, 'c', [(0, 1), (1, 0)])]
    all_to_all x1, starting transfers between devices: 6.47 us -> 4.25 us  [exchange(): return lax.all_to_all(v, axes, 0, 0, tiled=True)]
    pallas_call x4 -> x5, Pallas kernels: 9.43 us -> 9.64 us  [call(): pl.pallas_call(kernel, out_shape=shapes, in_specs=in_specs, out_specs=[VM...]
  transfers between devices with their start and end apart: 4 -> 5, of which waited for: 2 -> 3; matrix products, arithmetic and copies ran while one was open for 0% -> 0% of each run, Pallas kernels for 4% -> 3%
where the time goes in v5:
time: 134 us
  blocking collectives  84.6 us (63%)
  starting transfers between devices  14.3 us (11%)
  between operations  14.1 us (11%)
  waiting for transfers between devices  11.2 us (8%)
  Pallas kernels  9.64 us (7%)
    all_to_all x2, blocking collectives, exchange(): return lax.all_to_all(v, axes, 0, 0, tiled=True)  84.6 us
    pallas_call x5, Pallas kernels, call(): pl.pallas_call(kernel, out_shape=shapes, in_specs=in_specs, out_specs=[VM...  9.64 us
    all_to_all x1, waiting for transfers between devices, exchange(): return lax.all_to_all(v, axes, 0, 0, tiled=True)  8.7 us
    ppermute x1, starting transfers between devices, shards(): theirs = lax.ppermute(mine, 'c', [(0, 1), (1, 0)])  5.75 us
    all_to_all x1, starting transfers between devices, exchange(): return lax.all_to_all(v, axes, 0, 0, tiled=True)  4.25 us
    ppermute x1, starting transfers between devices, shards(): lax.ppermute(send, 'c', [(0, 1), (1, 0)])  3.61 us
  transfers between devices with their start and end apart: 5, of which 3 were waited for; matrix products, arithmetic and copies ran while one was open for 0% of the time, Pallas kernels for 3%

profile of v5, /device:TPU:1, one launch (start us, length us, event | category | flops | bytes accessed | tf_op | source)
XLA Modules:
  0.0 133.9 jit_solution(14769706867162030415)
XLA Ops:
  6.5 0.0 all-gather.3.cloned.1.call-start
  6.5 1.0 shard_map.55
  7.6 0.0 all-gather.3.cloned.1.call-update
  7.6 0.7 collective-permute-start
  8.3 0.0 collective-permute-done
  8.3 0.1 broadcast_in_dim.2
  8.4 37.8 %all_to_all.15.own_ref = bf16[32,64,128]{2,1,0:T(8,128)(2,1)S(1)} all-to-all(bf16[32,64,128]{2,1,0:T(8,128)(2,1)S(1)} %broadcast_in_dim.2), channel_id=1, replica_groups=mesh['z'=8,'y'=8,'x'=4,'c'=2] {'y','x'}, dimensions={0} | all-to-all | bytes 1048576 | tf_op jit(solution)/shard_map/all_to_all | solution.py:164
  46.2 5.8 %collective-permute-start.1 = (bf16[32,64,128]{2,1,0:T(8,128)(2,1)S(1)}, bf16[32,64,128]{2,1,0:T(8,128)(2,1)S(1)}, u32[]{:S(2)}, u32[]{:S(2)}) collective-permute-start(bf16[32,64,128]{2,1,0:T(8,128)(2,1)S(1)} %all_to_all.15.own_ref), channel_id=1, source_target_pairs={{0,1},{1,0},{2,3},{3,2},{4,5},{5,4},{6,7},{7,6},{8,9},{9,8},{10,11... | collective-permute-start | bytes 1572872 | tf_op jit(solution)/shard_map/ppermute | solution.py:173
  52.0 1.5 %collective-permute-done.1.other_ref = bf16[32,64,128]{2,1,0:T(8,128)(2,1)S(1)} collective-permute-done((bf16[32,64,128]{2,1,0:T(8,128)(2,1)S(1)}, bf16[32,64,128]{2,1,0:T(8,128)(2,1)S(1)}, u32[]{:S(2)}, u32[]{:S(2)}) %collective-permute-start.1) | collective-permute-done | bytes 524320 | tf_op jit(solution)/shard_map/ppermute | solution.py:173
  53.5 3.7 %shard_map.56 = bf16[8,64,1536]{2,1,0:T(8,128)(2,1)S(1)} custom-call(s32[1]{0:T(128)} %bitcast.core_ref, bf16[32,64,128]{2,1,0:T(8,128)(2,1)S(1)} %all_to_all.15.own_ref, bf16[32,64,128]{2,1,0:T(8,128)(2,1)S(1)} %collective-permute-done.1.other_ref, bf16[1024,1536]{1,0:T(8,128)(2,1)} %head_ref.1), custom_call_target="tpu_custom_call" | custom-call | tf_op jit(solution)/shard_map/pallas_call | solution.py:27
  57.2 46.8 %all_to_all.16.parts_ref = bf16[8,64,1536]{2,1,0:T(8,128)(2,1)S(1)} all-to-all(bf16[8,64,1536]{2,1,0:T(8,128)(2,1)S(1)} %shard_map.56), channel_id=1, replica_groups=mesh['z'=8,'y'=8,'x'=4,'c'=2] {'z'}, dimensions={0} | all-to-all | bytes 3145728 | tf_op jit(solution)/shard_map/all_to_all | solution.py:164
  104.0 0.0 all-gather.3.cloned.1.call-done
  104.0 3.4 %shard_map.57 = (bf16[32,16,128]{2,1,0:T(8,128)(2,1)S(1)}, bf16[32,16,128]{2,1,0:T(8,128)(2,1)S(1)}) custom-call(s32[1]{0:T(128)} %bitcast.core_ref, bf16[8,64,1536]{2,1,0:T(8,128)(2,1)S(1)} %all_to_all.16.parts_ref, bf16[8,1536,128]{2,1,0:T(8,128)(2,1)} %bitcast.4), custom_call_target="tpu_custom_call" | custom-call | tf_op jit(solution)/shard_map/pallas_call | solution.py:27
  107.4 3.6 %collective-permute-start.2 = (bf16[32,16,128]{2,1,0:T(8,128)(2,1)S(1)}, bf16[32,16,128]{2,1,0:T(8,128)(2,1)S(1)}, u32[]{:S(2)}, u32[]{:S(2)}) collective-permute-start(bf16[32,16,128]{2,1,0:T(8,128)(2,1)S(1)} %get-tuple-element.12), channel_id=1, source_target_pairs={{0,1},{1,0},{2,3},{3,2},{4,5},{5,4},{6,7},{7,6},{8,9},{9,8},{10,11... | collective-permute-start | bytes 393224 | tf_op jit(solution)/shard_map/ppermute | solution.py:197
  111.0 1.0 collective-permute-done.2.recv_ref
  112.0 0.8 shard_map.58
  112.7 4.3 %all-to-all-start.2 = ((bf16[32,16,128]{2,1,0:T(8,128)(2,1)}), bf16[32,16,128]{2,1,0:T(8,128)(2,1)S(1)}, u32[]{:S(2)}, u32[]{:S(2)}) async-start(bf16[32,16,128]{2,1,0:T(8,128)(2,1)} %shard_map.58), calls=%async_computation.2 | async-start | bytes 262144 | tf_op jit(solution)/shard_map/all_to_all | solution.py:164
  117.6 8.7 %all-to-all-done.2.in_ref = bf16[32,16,128]{2,1,0:T(8,128)(2,1)S(1)} async-done(((bf16[32,16,128]{2,1,0:T(8,128)(2,1)}), bf16[32,16,128]{2,1,0:T(8,128)(2,1)S(1)}, u32[]{:S(2)}, u32[]{:S(2)}) %all-to-all-start.2) | async-done | bytes 131104 | tf_op jit(solution)/shard_map/all_to_all | solution.py:164
  126.3 0.8 shard_map.59
Async XLA Ops:
  6.5 97.5 %all-gather.3.cloned.1.call-start = ((), (), s32[]{:S(2)}) async-start(), calls=%async_computation.3 | async-start | bytes 3538944 | tf_op jit(solution)/shard_map/all_gather | solution.py:169
  7.6 0.7 collective-permute-start
  46.2 7.3 %collective-permute-start.1 = (bf16[32,64,128]{2,1,0:T(8,128)(2,1)S(1)}, bf16[32,64,128]{2,1,0:T(8,128)(2,1)S(1)}, u32[]{:S(2)}, u32[]{:S(2)}) collective-permute-start(bf16[32,64,128]{2,1,0:T(8,128)(2,1)S(1)} %all_to_all.15.own_ref), channel_id=1, source_target_pairs={{0,1},{1,0},{2,3},{3,2},{4,5},{5,4},{6,7},{7,6},{8,9},{9,8},{10,11... | collective-permute-start | bytes 1572872 | tf_op jit(solution)/shard_map/ppermute | solution.py:173
  107.4 4.6 %collective-permute-start.2 = (bf16[32,16,128]{2,1,0:T(8,128)(2,1)S(1)}, bf16[32,16,128]{2,1,0:T(8,128)(2,1)S(1)}, u32[]{:S(2)}, u32[]{:S(2)}) collective-permute-start(bf16[32,16,128]{2,1,0:T(8,128)(2,1)S(1)} %get-tuple-element.12), channel_id=1, source_target_pairs={{0,1},{1,0},{2,3},{3,2},{4,5},{5,4},{6,7},{7,6},{8,9},{9,8},{10,11... | collective-permute-start | bytes 393224 | tf_op jit(solution)/shard_map/ppermute | solution.py:197
  112.7 13.6 %all-to-all-start.2 = ((bf16[32,16,128]{2,1,0:T(8,128)(2,1)}), bf16[32,16,128]{2,1,0:T(8,128)(2,1)S(1)}, u32[]{:S(2)}, u32[]{:S(2)}) async-start(bf16[32,16,128]{2,1,0:T(8,128)(2,1)} %shard_map.58), calls=%async_computation.2 | async-start | bytes 262144 | tf_op jit(solution)/shard_map/all_to_all | solution.py:164
Sparse Core Ops, SparseCore 0:
  9.4 53.6 all-gather.2

commit v6 on v5

--- a/solution.py
+++ b/solution.py
@@ -15,7 +15,7 @@
 STAY = pl.BlockSpec(memory_space=pl.ANY)
 
 
-def call(kernel, out_shape, in_specs, *args, scratch=(), out_memory=pltpu.VMEM):
+def call(kernel, out_shape, in_specs, *args, scratch=(), out_memory=pltpu.VMEM, limit=None):
     args = [
         pltpu.with_memory_space_constraint(a, pltpu.VMEM) if spec is VMEM else a
         for a, spec in zip(args, in_specs)
@@ -30,6 +30,7 @@
         in_specs=in_specs,
         out_specs=[VMEM] * len(out_shape) if isinstance(out_shape, list) else VMEM,
         scratch_shapes=list(scratch),
+        compiler_params=pltpu.CompilerParams(vmem_limit_bytes=limit),
     )(*args)
 
 
@@ -49,12 +50,13 @@
     ).astype(BF16)
 
 
-def logits_kernel(core_ref, own_ref, other_ref, head_ref, out_ref, held_ref, sems):
-    copies = [
-        pltpu.make_async_copy(head_ref.at[:, pl.ds(n * 256, 256)], held_ref.at[n], sems.at[n]) for n in range(6)
-    ]
-    for copy in copies:
-        copy.start()
+def hold_kernel(head_ref, out_ref, sem):
+    copy = pltpu.make_async_copy(head_ref, out_ref, sem)
+    copy.start()
+    copy.wait()
+
+
+def logits_kernel(core_ref, own_ref, other_ref, head_ref, out_ref):
     first = core_ref[0] == 0
     lhs = []
     for group in range(2):
@@ -68,9 +70,8 @@
             features.append(jnp.where(first, other, own))
         lhs.append(jnp.concatenate(features, axis=1))
     for n in range(6):
-        copies[n].wait()
         for group in range(2):
-            part = jnp.dot(lhs[group], held_ref[n], preferred_element_type=F32).astype(BF16)
+            part = jnp.dot(lhs[group], head_ref[:, n * 256 : n * 256 + 256], preferred_element_type=F32).astype(BF16)
             for owner in range(4):
                 out_ref[group * 4 + owner, :, pl.ds(n * 256, 256)] = part[owner * 64 : owner * 64 + 64]
 
@@ -155,7 +156,7 @@
     expected = pltpu.roll(jnp.broadcast_to(weighted / denominator, (8, 128)), 64, 1)[0:1]
     row, lane = iota((16, 128), 0), iota((16, 128), 1)
     column = jnp.sum(jnp.where(lane == row + 64, sums, 0.0), axis=1, keepdims=True)
-    result = jnp.where(lane < count_ref[0], total - expected * column, 0.0)
+    result = jnp.where(lane < count_ref[...], total - expected * column, 0.0)
     out_ref[...] = result[:, 0:64]
 
 
@@ -171,15 +172,23 @@
     moved = lax.ppermute(owned, ("z", "y", "x", "c"), pairs)
     mine = exchange(jnp.broadcast_to(moved[None], (32, 64, 128)), ("y", "x"))
     theirs = lax.ppermute(mine, "c", [(0, 1), (1, 0)])
+    held = call(
+        hold_kernel,
+        ((1024, 1536), BF16),
+        [STAY],
+        head_weight,
+        scratch=[pltpu.SemaphoreType.DMA],
+        limit=58 << 20,
+    )
     parts = call(
         logits_kernel,
         ((8, 64, 1536), BF16),
-        [SMEM, VMEM, VMEM, STAY],
+        [SMEM, VMEM, VMEM, VMEM],
         core,
         mine,
         theirs,
-        head_weight,
-        scratch=[pltpu.VMEM((6, 1024, 256), BF16), pltpu.SemaphoreType.DMA((6,))],
+        held,
+        limit=32 << 20,
     )
     keep, send = call(
         project_kernel,
@@ -196,7 +205,7 @@
     )
     tiles = call(pair_kernel, ((32, 16, 128), BF16), [VMEM, VMEM], keep, lax.ppermute(send, "c", [(0, 1), (1, 0)]))
     tiles = exchange(tiles, ("y", "x"))
-    return call(finish_kernel, ((16, 64), F32), [SMEM, VMEM], counts, tiles, out_memory=None).T
+    return call(finish_kernel, ((16, 64), F32), [OUTER, VMEM], counts.reshape(1, 1), tiles, out_memory=None).T
 
 
 def solution(mesh):

time: 134 us -> 133 us (level)
  waiting for transfers between devices: 11.2 us -> 9.69 us
    ppermute x1, waiting for transfers between devices: 1.51 us -> 0.01 us  [shards(): theirs = lax.ppermute(mine, 'c', [(0, 1), (1, 0)])]
    pallas_call x5 -> x6, Pallas kernels: 9.64 us -> 9.63 us  [call(): pl.pallas_call(kernel, out_shape=shapes, in_specs=in_specs, out_specs=[VM...]
  transfers between devices with their start and end apart: 5 -> 5, of which waited for: 3 -> 2; matrix products, arithmetic and copies ran while one was open for 0% -> 0% of each run, Pallas kernels for 3% -> 3%
where the time goes in v6:
time: 133 us; the launch traced here: 132 us
  blocking collectives  85.8 us (65%)
  between operations  14.1 us (11%)
  starting transfers between devices  13 us (10%)
  waiting for transfers between devices  9.69 us (7%)
  Pallas kernels  9.63 us (7%)
    all_to_all x2, blocking collectives, exchange(): return lax.all_to_all(v, axes, 0, 0, tiled=True)  85.8 us
    pallas_call x6, Pallas kernels, call(): pl.pallas_call(kernel, out_shape=shapes, in_specs=in_specs, out_specs=[VM...  9.63 us
    all_to_all x1, waiting for transfers between devices, exchange(): return lax.all_to_all(v, axes, 0, 0, tiled=True)  8.7 us
    ppermute x1, starting transfers between devices, shards(): theirs = lax.ppermute(mine, 'c', [(0, 1), (1, 0)])  5.75 us
    all_to_all x1, starting transfers between devices, exchange(): return lax.all_to_all(v, axes, 0, 0, tiled=True)  4.26 us
  transfers between devices with their start and end apart: 5, of which 2 were waited for; matrix products, arithmetic and copies ran while one was open for 0% of the time, Pallas kernels for 3%

profile of v6, /device:TPU:1, one launch (start us, length us, event | category | flops | bytes accessed | tf_op | source)
XLA Modules:
  0.0 132.4 jit_solution(10348059410930765550)
XLA Ops:
  6.5 0.0 all-gather.3.cloned.1.call-start
  6.5 1.0 shard_map.55
  7.6 0.0 all-gather.3.cloned.1.call-update
  7.6 0.7 collective-permute-start
  8.3 0.0 collective-permute-done
  8.3 0.1 broadcast_in_dim.2
  8.4 37.8 %all_to_all.15.own_ref = bf16[32,64,128]{2,1,0:T(8,128)(2,1)S(1)} all-to-all(bf16[32,64,128]{2,1,0:T(8,128)(2,1)S(1)} %broadcast_in_dim.2), channel_id=1, replica_groups=mesh['z'=8,'y'=8,'x'=4,'c'=2] {'y','x'}, dimensions={0} | all-to-all | bytes 1048576 | tf_op jit(solution)/shard_map/all_to_all | solution.py:165
  46.2 5.8 %collective-permute-start.1 = (bf16[32,64,128]{2,1,0:T(8,128)(2,1)S(1)}, bf16[32,64,128]{2,1,0:T(8,128)(2,1)S(1)}, u32[]{:S(2)}, u32[]{:S(2)}) collective-permute-start(bf16[32,64,128]{2,1,0:T(8,128)(2,1)S(1)} %all_to_all.15.own_ref), channel_id=1, source_target_pairs={{0,1},{1,0},{2,3},{3,2},{4,5},{5,4},{6,7},{7,6},{8,9},{9,8},{10,11... | collective-permute-start | bytes 1572872 | tf_op jit(solution)/shard_map/ppermute | solution.py:174
  52.0 1.9 %shard_map.56.head_ref = bf16[1024,1536]{1,0:T(8,128)(2,1)S(1)} custom-call(bf16[1024,1536]{1,0:T(8,128)(2,1)} %head_ref.1), custom_call_target="tpu_custom_call" | custom-call | tf_op jit(solution)/shard_map/pallas_call | solution.py:27
  53.9 0.0 collective-permute-done.1.other_ref
  53.9 1.8 %shard_map.57 = bf16[8,64,1536]{2,1,0:T(8,128)(2,1)S(1)} custom-call(s32[1]{0:T(128)} %bitcast.1.core_ref, bf16[32,64,128]{2,1,0:T(8,128)(2,1)S(1)} %all_to_all.15.own_ref, bf16[32,64,128]{2,1,0:T(8,128)(2,1)S(1)} %collective-permute-done.1.other_ref, bf16[1024,1536]{1,0:T(8,128)(2,1)S(1)} %shard_map.56.head_ref), custom_call_target="tpu_custom_call" | custom-call | tf_op jit(solution)/shard_map/pallas_call | solution.py:27
  55.7 48.0 %all_to_all.16.parts_ref = bf16[8,64,1536]{2,1,0:T(8,128)(2,1)S(1)} all-to-all(bf16[8,64,1536]{2,1,0:T(8,128)(2,1)S(1)} %shard_map.57), channel_id=1, replica_groups=mesh['z'=8,'y'=8,'x'=4,'c'=2] {'z'}, dimensions={0} | all-to-all | bytes 3145728 | tf_op jit(solution)/shard_map/all_to_all | solution.py:165
  103.7 0.0 all-gather.3.cloned.1.call-done
  103.8 3.4 %shard_map.58 = (bf16[32,16,128]{2,1,0:T(8,128)(2,1)S(1)}, bf16[32,16,128]{2,1,0:T(8,128)(2,1)S(1)}) custom-call(s32[1]{0:T(128)} %bitcast.1.core_ref, bf16[8,64,1536]{2,1,0:T(8,128)(2,1)S(1)} %all_to_all.16.parts_ref, bf16[8,1536,128]{2,1,0:T(8,128)(2,1)} %bitcast.6), custom_call_target="tpu_custom_call" | custom-call | tf_op jit(solution)/shard_map/pallas_call | solution.py:27
  107.1 2.4 %collective-permute-start.2 = (bf16[32,16,128]{2,1,0:T(8,128)(2,1)S(1)}, bf16[32,16,128]{2,1,0:T(8,128)(2,1)S(1)}, u32[]{:S(2)}, u32[]{:S(2)}) collective-permute-start(bf16[32,16,128]{2,1,0:T(8,128)(2,1)S(1)} %get-tuple-element.12), channel_id=1, source_target_pairs={{0,1},{1,0},{2,3},{3,2},{4,5},{5,4},{6,7},{7,6},{8,9},{9,8},{10,11... | collective-permute-start | bytes 393224 | tf_op jit(solution)/shard_map/ppermute | solution.py:206
  109.5 1.0 collective-permute-done.2.recv_ref
  110.5 0.8 shard_map.59
  111.2 4.3 %all-to-all-start.2 = ((bf16[32,16,128]{2,1,0:T(8,128)(2,1)}), bf16[32,16,128]{2,1,0:T(8,128)(2,1)S(1)}, u32[]{:S(2)}, u32[]{:S(2)}) async-start(bf16[32,16,128]{2,1,0:T(8,128)(2,1)} %shard_map.59), calls=%async_computation.2 | async-start | bytes 262144 | tf_op jit(solution)/shard_map/all_to_all | solution.py:165
  116.1 8.7 %all-to-all-done.2.in_ref = bf16[32,16,128]{2,1,0:T(8,128)(2,1)S(1)} async-done(((bf16[32,16,128]{2,1,0:T(8,128)(2,1)}), bf16[32,16,128]{2,1,0:T(8,128)(2,1)S(1)}, u32[]{:S(2)}, u32[]{:S(2)}) %all-to-all-start.2) | async-done | bytes 131104 | tf_op jit(solution)/shard_map/all_to_all | solution.py:165
  124.8 0.8 shard_map.60
Async XLA Ops:
  6.5 97.2 %all-gather.3.cloned.1.call-start = ((), (), s32[]{:S(2)}) async-start(), calls=%async_computation.3 | async-start | bytes 3538944 | tf_op jit(solution)/shard_map/all_gather | solution.py:170
  7.6 0.7 collective-permute-start
  46.2 7.7 %collective-permute-start.1 = (bf16[32,64,128]{2,1,0:T(8,128)(2,1)S(1)}, bf16[32,64,128]{2,1,0:T(8,128)(2,1)S(1)}, u32[]{:S(2)}, u32[]{:S(2)}) collective-permute-start(bf16[32,64,128]{2,1,0:T(8,128)(2,1)S(1)} %all_to_all.15.own_ref), channel_id=1, source_target_pairs={{0,1},{1,0},{2,3},{3,2},{4,5},{5,4},{6,7},{7,6},{8,9},{9,8},{10,11... | collective-permute-start | bytes 1572872 | tf_op jit(solution)/shard_map/ppermute | solution.py:174
  107.1 3.3 %collective-permute-start.2 = (bf16[32,16,128]{2,1,0:T(8,128)(2,1)S(1)}, bf16[32,16,128]{2,1,0:T(8,128)(2,1)S(1)}, u32[]{:S(2)}, u32[]{:S(2)}) collective-permute-start(bf16[32,16,128]{2,1,0:T(8,128)(2,1)S(1)} %get-tuple-element.12), channel_id=1, source_target_pairs={{0,1},{1,0},{2,3},{3,2},{4,5},{5,4},{6,7},{7,6},{8,9},{9,8},{10,11... | collective-permute-start | bytes 393224 | tf_op jit(solution)/shard_map/ppermute | solution.py:206
  111.2 13.6 %all-to-all-start.2 = ((bf16[32,16,128]{2,1,0:T(8,128)(2,1)}), bf16[32,16,128]{2,1,0:T(8,128)(2,1)S(1)}, u32[]{:S(2)}, u32[]{:S(2)}) async-start(bf16[32,16,128]{2,1,0:T(8,128)(2,1)} %shard_map.59), calls=%async_computation.2 | async-start | bytes 262144 | tf_op jit(solution)/shard_map/all_to_all | solution.py:165
Sparse Core Ops, SparseCore 0:
  9.4 53.6 all-gather.2

commit v7 on v6

--- a/solution.py
+++ b/solution.py
@@ -50,7 +50,8 @@
     ).astype(BF16)
 
 
-def hold_kernel(head_ref, out_ref, sem):
+def hold_kernel(head_ref, count_ref, out_ref, live_ref, sem):
+    live_ref[...] = jnp.broadcast_to(count_ref[...], (8, 128))
     copy = pltpu.make_async_copy(head_ref, out_ref, sem)
     copy.start()
     copy.wait()
@@ -63,7 +64,7 @@
         rows = pl.ds(group * 256, 256)
         features = []
         for x in range(4):
-            picks = [16 * group + 4 * o + x for o in range(4)]
+            picks = [16 * (1 - group) + 4 * o + x for o in range(4)]
             own = jnp.concatenate([own_ref[p] for p in picks], axis=0)
             other = jnp.concatenate([other_ref[p] for p in picks], axis=0)
             features.append(jnp.where(first, own, other))
@@ -156,7 +157,7 @@
     expected = pltpu.roll(jnp.broadcast_to(weighted / denominator, (8, 128)), 64, 1)[0:1]
     row, lane = iota((16, 128), 0), iota((16, 128), 1)
     column = jnp.sum(jnp.where(lane == row + 64, sums, 0.0), axis=1, keepdims=True)
-    result = jnp.where(lane < count_ref[...], total - expected * column, 0.0)
+    result = jnp.where(lane < count_ref[0:1, :], total - expected * column, 0.0)
     out_ref[...] = result[:, 0:64]
 
 
@@ -168,15 +169,16 @@
     owned = call(select_kernel, ((64, 128), BF16), [OUTER, OUTER], keep_index.reshape(1, 64), hidden)
     late_basis, owned = lax.optimization_barrier((vocab_basis, owned))
     basis = lax.all_gather(late_basis, "z")
-    pairs = [((z * 8 + y) * 8 + k, (y * 8 + z) * 8 + k) for z in range(8) for y in range(8) for k in range(8)]
+    pairs = [((z * 8 + y) * 8 + k, (y * 8 + (z + 4) % 8) * 8 + k) for z in range(8) for y in range(8) for k in range(8)]
     moved = lax.ppermute(owned, ("z", "y", "x", "c"), pairs)
     mine = exchange(jnp.broadcast_to(moved[None], (32, 64, 128)), ("y", "x"))
     theirs = lax.ppermute(mine, "c", [(0, 1), (1, 0)])
-    held = call(
+    held, live = call(
         hold_kernel,
-        ((1024, 1536), BF16),
-        [STAY],
+        [((1024, 1536), BF16), ((8, 128), jnp.int32)],
+        [STAY, OUTER],
         head_weight,
+        counts.reshape(1, 1),
         scratch=[pltpu.SemaphoreType.DMA],
         limit=58 << 20,
     )
@@ -205,7 +207,7 @@
     )
     tiles = call(pair_kernel, ((32, 16, 128), BF16), [VMEM, VMEM], keep, lax.ppermute(send, "c", [(0, 1), (1, 0)]))
     tiles = exchange(tiles, ("y", "x"))
-    return call(finish_kernel, ((16, 64), F32), [OUTER, VMEM], counts.reshape(1, 1), tiles, out_memory=None).T
+    return call(finish_kernel, ((16, 64), F32), [VMEM, VMEM], live, tiles, out_memory=None).T
 
 
 def solution(mesh):

time: 133 us -> 132 us (level)
  waiting for transfers between devices: 9.69 us -> 5.28 us
  starting transfers between devices: 13 us -> 16.1 us
    all_to_all x1 -> x0, waiting for transfers between devices: 8.7 us -> none  [exchange(): return lax.all_to_all(v, axes, 0, 0, tiled=True)]
    ppermute x1, starting transfers between devices: 0.66 us -> 8.27 us  [shards(): moved = lax.ppermute(owned, ('z', 'y', 'x', 'c'), pairs)]
    ppermute x1, waiting for transfers between devices: 0.01 us -> 4.3 us  [shards(): moved = lax.ppermute(owned, ('z', 'y', 'x', 'c'), pairs)]
    all_to_all x1 -> x0, starting transfers between devices: 4.26 us -> none  [exchange(): return lax.all_to_all(v, axes, 0, 0, tiled=True)]
    all_to_all x2 -> x3, blocking collectives: 85.8 us -> 87 us  [exchange(): return lax.all_to_all(v, axes, 0, 0, tiled=True)]
  transfers between devices with their start and end apart: 5 -> 4, of which waited for: 2 -> 2; matrix products, arithmetic and copies ran while one was open for 0% -> 0% of each run, Pallas kernels for 3% -> 3%
where the time goes in v7:
time: 132 us
  blocking collectives  87 us (66%)
  starting transfers between devices  16.1 us (12%)
  between operations  14.1 us (11%)
  Pallas kernels  9 us (7%)
  waiting for transfers between devices  5.28 us (4%)
    all_to_all x3, blocking collectives, exchange(): return lax.all_to_all(v, axes, 0, 0, tiled=True)  87 us
    pallas_call x6, Pallas kernels, call(): pl.pallas_call(kernel, out_shape=shapes, in_specs=in_specs, out_specs=[VM...  9 us
    ppermute x1, starting transfers between devices, shards(): moved = lax.ppermute(owned, ('z', 'y', 'x', 'c'), pairs)  8.27 us
    ppermute x1, starting transfers between devices, shards(): theirs = lax.ppermute(mine, 'c', [(0, 1), (1, 0)])  5.47 us
    ppermute x1, waiting for transfers between devices, shards(): moved = lax.ppermute(owned, ('z', 'y', 'x', 'c'), pairs)  4.3 us
  transfers between devices with their start and end apart: 4, of which 2 were waited for; matrix products, arithmetic and copies ran while one was open for 0% of the time, Pallas kernels for 3%

profile of v7, /device:TPU:1, one launch (start us, length us, event | category | flops | bytes accessed | tf_op | source)
XLA Modules:
  0.0 131.6 jit_solution(15421125564660827982)
XLA Ops:
  6.5 0.0 all-gather.3.cloned.1.call-start
  6.5 1.0 shard_map.56
  7.6 0.0 all-gather.3.cloned.1.call-update
  7.6 8.3 %collective-permute-start = (bf16[64,128]{1,0:T(8,128)(2,1)S(1)}, bf16[64,128]{1,0:T(8,128)(2,1)S(1)}, u32[]{:S(2)}, u32[]{:S(2)}) collective-permute-start(bf16[64,128]{1,0:T(8,128)(2,1)S(1)} %shard_map.56), channel_id=1, source_target_pairs={{0,32},{1,33},{2,34},{3,35},{4,36},{5,37},{6,38},{7,39},{8,96},{9,... | collective-permute-start | bytes 49160 | tf_op jit(solution)/shard_map/ppermute | solution.py:173
  15.9 4.3 %collective-permute-done = bf16[64,128]{1,0:T(8,128)(2,1)S(1)} collective-permute-done((bf16[64,128]{1,0:T(8,128)(2,1)S(1)}, bf16[64,128]{1,0:T(8,128)(2,1)S(1)}, u32[]{:S(2)}, u32[]{:S(2)}) %collective-permute-start) | collective-permute-done | bytes 16416 | tf_op jit(solution)/shard_map/ppermute | solution.py:173
  20.2 0.1 broadcast_in_dim.2
  20.3 24.5 %all_to_all.15.own_ref = bf16[32,64,128]{2,1,0:T(8,128)(2,1)S(1)} all-to-all(bf16[32,64,128]{2,1,0:T(8,128)(2,1)S(1)} %broadcast_in_dim.2), channel_id=1, replica_groups=mesh['z'=8,'y'=8,'x'=4,'c'=2] {'y','x'}, dimensions={0} | all-to-all | bytes 1048576 | tf_op jit(solution)/shard_map/all_to_all | solution.py:166
  44.8 5.5 %collective-permute-start.1 = (bf16[32,64,128]{2,1,0:T(8,128)(2,1)S(1)}, bf16[32,64,128]{2,1,0:T(8,128)(2,1)S(1)}, u32[]{:S(2)}, u32[]{:S(2)}) collective-permute-start(bf16[32,64,128]{2,1,0:T(8,128)(2,1)S(1)} %all_to_all.15.own_ref), channel_id=1, source_target_pairs={{0,1},{1,0},{2,3},{3,2},{4,5},{5,4},{6,7},{7,6},{8,9},{9,8},{10,11... | collective-permute-start | bytes 1572872 | tf_op jit(solution)/shard_map/ppermute | solution.py:175
  50.9 1.9 %shard_map.55 = (bf16[1024,1536]{1,0:T(8,128)(2,1)S(1)}, s32[8,128]{1,0:T(8,128)S(1)}) custom-call(bf16[1024,1536]{1,0:T(8,128)(2,1)} %head_ref.1, s32[1,1]{1,0:T(1,128)} %bitcast.5.count_ref), custom_call_target="tpu_custom_call" | custom-call | tf_op jit(solution)/shard_map/pallas_call | solution.py:27
  52.8 0.0 collective-permute-done.1.other_ref
  52.8 1.8 %shard_map.57 = bf16[8,64,1536]{2,1,0:T(8,128)(2,1)S(1)} custom-call(s32[1]{0:T(128)} %bitcast.1.core_ref, bf16[32,64,128]{2,1,0:T(8,128)(2,1)S(1)} %all_to_all.15.own_ref, bf16[32,64,128]{2,1,0:T(8,128)(2,1)S(1)} %collective-permute-done.1.other_ref, bf16[1024,1536]{1,0:T(8,128)(2,1)S(1)} %get-tuple-element.13.head_ref), custom_call_target="tpu_custom_call" | custom-call | tf_op jit(solution)/shard_map/pallas_call | solution.py:27
  54.7 47.2 %all_to_all.16.parts_ref = bf16[8,64,1536]{2,1,0:T(8,128)(2,1)S(1)} all-to-all(bf16[8,64,1536]{2,1,0:T(8,128)(2,1)S(1)} %shard_map.57), channel_id=1, replica_groups=mesh['z'=8,'y'=8,'x'=4,'c'=2] {'z'}, dimensions={0} | all-to-all | bytes 3145728 | tf_op jit(solution)/shard_map/all_to_all | solution.py:166
  101.8 0.0 all-gather.3.cloned.1.call-done
  101.8 3.4 %shard_map.58 = (bf16[32,16,128]{2,1,0:T(8,128)(2,1)S(1)}, bf16[32,16,128]{2,1,0:T(8,128)(2,1)S(1)}) custom-call(s32[1]{0:T(128)} %bitcast.1.core_ref, bf16[8,64,1536]{2,1,0:T(8,128)(2,1)S(1)} %all_to_all.16.parts_ref, bf16[8,1536,128]{2,1,0:T(8,128)(2,1)} %bitcast.6), custom_call_target="tpu_custom_call" | custom-call | tf_op jit(solution)/shard_map/pallas_call | solution.py:27
  105.2 2.4 %collective-permute-start.2 = (bf16[32,16,128]{2,1,0:T(8,128)(2,1)S(1)}, bf16[32,16,128]{2,1,0:T(8,128)(2,1)S(1)}, u32[]{:S(2)}, u32[]{:S(2)}) collective-permute-start(bf16[32,16,128]{2,1,0:T(8,128)(2,1)S(1)} %get-tuple-element.16), channel_id=1, source_target_pairs={{0,1},{1,0},{2,3},{3,2},{4,5},{5,4},{6,7},{7,6},{8,9},{9,8},{10,11... | collective-permute-start | bytes 393224 | tf_op jit(solution)/shard_map/ppermute | solution.py:208
  107.6 1.0 collective-permute-done.2.recv_ref
  108.5 0.1 shard_map.59
  108.6 15.3 %all_to_all.17.in_ref = bf16[32,16,128]{2,1,0:T(8,128)(2,1)S(1)} all-to-all(bf16[32,16,128]{2,1,0:T(8,128)(2,1)S(1)} %shard_map.59), channel_id=1, replica_groups=mesh['z'=8,'y'=8,'x'=4,'c'=2] {'y','x'}, dimensions={0} | all-to-all | bytes 262144 | tf_op jit(solution)/shard_map/all_to_all | solution.py:166
  124.0 0.8 shard_map.60
Async XLA Ops:
  6.5 95.3 %all-gather.3.cloned.1.call-start = ((), (), s32[]{:S(2)}) async-start(), calls=%async_computation.3 | async-start | bytes 3538944 | tf_op jit(solution)/shard_map/all_gather | solution.py:171
  7.6 12.6 %collective-permute-start = (bf16[64,128]{1,0:T(8,128)(2,1)S(1)}, bf16[64,128]{1,0:T(8,128)(2,1)S(1)}, u32[]{:S(2)}, u32[]{:S(2)}) collective-permute-start(bf16[64,128]{1,0:T(8,128)(2,1)S(1)} %shard_map.56), channel_id=1, source_target_pairs={{0,32},{1,33},{2,34},{3,35},{4,36},{5,37},{6,38},{7,39},{8,96},{9,... | collective-permute-start | bytes 49160 | tf_op jit(solution)/shard_map/ppermute | solution.py:173
  44.8 8.1 %collective-permute-start.1 = (bf16[32,64,128]{2,1,0:T(8,128)(2,1)S(1)}, bf16[32,64,128]{2,1,0:T(8,128)(2,1)S(1)}, u32[]{:S(2)}, u32[]{:S(2)}) collective-permute-start(bf16[32,64,128]{2,1,0:T(8,128)(2,1)S(1)} %all_to_all.15.own_ref), channel_id=1, source_target_pairs={{0,1},{1,0},{2,3},{3,2},{4,5},{5,4},{6,7},{7,6},{8,9},{9,8},{10,11... | collective-permute-start | bytes 1572872 | tf_op jit(solution)/shard_map/ppermute | solution.py:175
  105.2 3.3 %collective-permute-start.2 = (bf16[32,16,128]{2,1,0:T(8,128)(2,1)S(1)}, bf16[32,16,128]{2,1,0:T(8,128)(2,1)S(1)}, u32[]{:S(2)}, u32[]{:S(2)}) collective-permute-start(bf16[32,16,128]{2,1,0:T(8,128)(2,1)S(1)} %get-tuple-element.16), channel_id=1, source_target_pairs={{0,1},{1,0},{2,3},{3,2},{4,5},{5,4},{6,7},{7,6},{8,9},{9,8},{10,11... | collective-permute-start | bytes 393224 | tf_op jit(solution)/shard_map/ppermute | solution.py:208
Sparse Core Ops, SparseCore 0:
  9.4 53.6 all-gather.2

commit v8 on v6

--- a/solution.py
+++ b/solution.py
@@ -50,6 +50,10 @@
     ).astype(BF16)
 
 
+def live_kernel(count_ref, out_ref):
+    out_ref[...] = jnp.broadcast_to(count_ref[...], (8, 128))
+
+
 def hold_kernel(head_ref, out_ref, sem):
     copy = pltpu.make_async_copy(head_ref, out_ref, sem)
     copy.start()
@@ -63,7 +67,7 @@
         rows = pl.ds(group * 256, 256)
         features = []
         for x in range(4):
-            picks = [16 * group + 4 * o + x for o in range(4)]
+            picks = [16 * (1 - group) + 4 * o + x for o in range(4)]
             own = jnp.concatenate([own_ref[p] for p in picks], axis=0)
             other = jnp.concatenate([other_ref[p] for p in picks], axis=0)
             features.append(jnp.where(first, own, other))
@@ -156,7 +160,7 @@
     expected = pltpu.roll(jnp.broadcast_to(weighted / denominator, (8, 128)), 64, 1)[0:1]
     row, lane = iota((16, 128), 0), iota((16, 128), 1)
     column = jnp.sum(jnp.where(lane == row + 64, sums, 0.0), axis=1, keepdims=True)
-    result = jnp.where(lane < count_ref[...], total - expected * column, 0.0)
+    result = jnp.where(lane < count_ref[0:1, :], total - expected * column, 0.0)
     out_ref[...] = result[:, 0:64]
 
 
@@ -166,10 +170,11 @@
 
     core = lax.axis_index("c").astype(jnp.int32).reshape(1)
     owned = call(select_kernel, ((64, 128), BF16), [OUTER, OUTER], keep_index.reshape(1, 64), hidden)
-    late_basis, owned = lax.optimization_barrier((vocab_basis, owned))
-    basis = lax.all_gather(late_basis, "z")
-    pairs = [((z * 8 + y) * 8 + k, (y * 8 + z) * 8 + k) for z in range(8) for y in range(8) for k in range(8)]
+    late_counts, owned = lax.optimization_barrier((counts, owned))
+    basis = lax.all_gather(vocab_basis, "z")
+    pairs = [((z * 8 + y) * 8 + k, (y * 8 + (z + 4) % 8) * 8 + k) for z in range(8) for y in range(8) for k in range(8)]
     moved = lax.ppermute(owned, ("z", "y", "x", "c"), pairs)
+    live = call(live_kernel, ((8, 128), jnp.int32), [OUTER], late_counts.reshape(1, 1))
     mine = exchange(jnp.broadcast_to(moved[None], (32, 64, 128)), ("y", "x"))
     theirs = lax.ppermute(mine, "c", [(0, 1), (1, 0)])
     held = call(
@@ -205,7 +210,7 @@
     )
     tiles = call(pair_kernel, ((32, 16, 128), BF16), [VMEM, VMEM], keep, lax.ppermute(send, "c", [(0, 1), (1, 0)]))
     tiles = exchange(tiles, ("y", "x"))
-    return call(finish_kernel, ((16, 64), F32), [OUTER, VMEM], counts.reshape(1, 1), tiles, out_memory=None).T
+    return call(finish_kernel, ((16, 64), F32), [VMEM, VMEM], live, tiles, out_memory=None).T
 
 
 def solution(mesh):

time: 133 us -> 133 us (level)
  blocking collectives: 85.8 us -> 71.6 us
  starting transfers between devices: 13 us -> 22.3 us
  waiting for transfers between devices: 9.69 us -> 14.6 us
    all_to_all x2, blocking collectives: 85.8 us -> 71.6 us  [exchange(): return lax.all_to_all(v, axes, 0, 0, tiled=True)]
    ppermute x1, starting transfers between devices: 0.66 us -> 8.27 us  [shards(): moved = lax.ppermute(owned, ('z', 'y', 'x', 'c'), pairs)]
    ppermute x1, waiting for transfers between devices: 0.01 us -> 4.3 us  [shards(): moved = lax.ppermute(owned, ('z', 'y', 'x', 'c'), pairs)]
    all_to_all x1, starting transfers between devices: 4.26 us -> 6.14 us  [exchange(): return lax.all_to_all(v, axes, 0, 0, tiled=True)]
    pallas_call x6 -> x7, Pallas kernels: 9.63 us -> 9.71 us  [call(): pl.pallas_call(kernel, out_shape=shapes, in_specs=in_specs, out_specs=[VM...]
  transfers between devices with their start and end apart: 5 -> 5, of which waited for: 2 -> 3; matrix products, arithmetic and copies ran while one was open for 0% -> 0% of each run, Pallas kernels for 3% -> 4%
where the time goes in v8:
time: 133 us; the launch traced here: 132 us
  blocking collectives  71.6 us (54%)
  starting transfers between devices  22.3 us (17%)
  waiting for transfers between devices  14.6 us (11%)
  between operations  14.1 us (11%)
  Pallas kernels  9.71 us (7%)
    all_to_all x2, blocking collectives, exchange(): return lax.all_to_all(v, axes, 0, 0, tiled=True)  71.6 us
    pallas_call x7, Pallas kernels, call(): pl.pallas_call(kernel, out_shape=shapes, in_specs=in_specs, out_specs=[VM...  9.71 us
    all_to_all x1, waiting for transfers between devices, exchange(): return lax.all_to_all(v, axes, 0, 0, tiled=True)  8.63 us
    ppermute x1, starting transfers between devices, shards(): moved = lax.ppermute(owned, ('z', 'y', 'x', 'c'), pairs)  8.27 us
    all_to_all x1, starting transfers between devices, exchange(): return lax.all_to_all(v, axes, 0, 0, tiled=True)  6.14 us
    ppermute x1, starting transfers between devices, shards(): theirs = lax.ppermute(mine, 'c', [(0, 1), (1, 0)])  5.47 us
    ppermute x1, waiting for transfers between devices, shards(): moved = lax.ppermute(owned, ('z', 'y', 'x', 'c'), pairs)  4.3 us
  transfers between devices with their start and end apart: 5, of which 3 were waited for; matrix products, arithmetic and copies ran while one was open for 0% of the time, Pallas kernels for 4%

profile of v8, /device:TPU:1, one launch (start us, length us, event | category | flops | bytes accessed | tf_op | source)
XLA Modules:
  0.0 132.4 jit_solution(16871814642881443735)
XLA Ops:
  6.5 0.0 all-gather.3.cloned.1.call-start
  6.5 0.7 all-gather.3.cloned.1.call-update
  7.3 1.0 shard_map.55
  8.3 8.3 %collective-permute-start = (bf16[64,128]{1,0:T(8,128)(2,1)S(1)}, bf16[64,128]{1,0:T(8,128)(2,1)S(1)}, u32[]{:S(2)}, u32[]{:S(2)}) collective-permute-start(bf16[64,128]{1,0:T(8,128)(2,1)S(1)} %shard_map.55), channel_id=1, source_target_pairs={{0,32},{1,33},{2,34},{3,35},{4,36},{5,37},{6,38},{7,39},{8,96},{9,... | collective-permute-start | bytes 49160 | tf_op jit(solution)/shard_map/ppermute | solution.py:176
  16.6 4.3 %collective-permute-done = bf16[64,128]{1,0:T(8,128)(2,1)S(1)} collective-permute-done((bf16[64,128]{1,0:T(8,128)(2,1)S(1)}, bf16[64,128]{1,0:T(8,128)(2,1)S(1)}, u32[]{:S(2)}, u32[]{:S(2)}) %collective-permute-start) | collective-permute-done | bytes 16416 | tf_op jit(solution)/shard_map/ppermute | solution.py:176
  20.9 0.1 broadcast_in_dim.2
  21.0 24.5 %all_to_all.15.own_ref = bf16[32,64,128]{2,1,0:T(8,128)(2,1)S(1)} all-to-all(bf16[32,64,128]{2,1,0:T(8,128)(2,1)S(1)} %broadcast_in_dim.2), channel_id=1, replica_groups=mesh['z'=8,'y'=8,'x'=4,'c'=2] {'y','x'}, dimensions={0} | all-to-all | bytes 1048576 | tf_op jit(solution)/shard_map/all_to_all | solution.py:169
  45.5 5.5 %collective-permute-start.1 = (bf16[32,64,128]{2,1,0:T(8,128)(2,1)S(1)}, bf16[32,64,128]{2,1,0:T(8,128)(2,1)S(1)}, u32[]{:S(2)}, u32[]{:S(2)}) collective-permute-start(bf16[32,64,128]{2,1,0:T(8,128)(2,1)S(1)} %all_to_all.15.own_ref), channel_id=1, source_target_pairs={{0,1},{1,0},{2,3},{3,2},{4,5},{5,4},{6,7},{7,6},{8,9},{9,8},{10,11... | collective-permute-start | bytes 1572872 | tf_op jit(solution)/shard_map/ppermute | solution.py:179
  50.9 1.9 %shard_map.57.head_ref = bf16[1024,1536]{1,0:T(8,128)(2,1)S(1)} custom-call(bf16[1024,1536]{1,0:T(8,128)(2,1)} %head_ref.1), custom_call_target="tpu_custom_call" | custom-call | tf_op jit(solution)/shard_map/pallas_call | solution.py:27
  52.9 0.0 collective-permute-done.1.other_ref
  52.9 1.8 %shard_map.58 = bf16[8,64,1536]{2,1,0:T(8,128)(2,1)S(1)} custom-call(s32[1]{0:T(128)} %bitcast.2.core_ref, bf16[32,64,128]{2,1,0:T(8,128)(2,1)S(1)} %all_to_all.15.own_ref, bf16[32,64,128]{2,1,0:T(8,128)(2,1)S(1)} %collective-permute-done.1.other_ref, bf16[1024,1536]{1,0:T(8,128)(2,1)S(1)} %shard_map.57.head_ref), custom_call_target="tpu_custom_call" | custom-call | tf_op jit(solution)/shard_map/pallas_call | solution.py:27
  54.7 47.2 %all_to_all.16.parts_ref = bf16[8,64,1536]{2,1,0:T(8,128)(2,1)S(1)} all-to-all(bf16[8,64,1536]{2,1,0:T(8,128)(2,1)S(1)} %shard_map.58), channel_id=1, replica_groups=mesh['z'=8,'y'=8,'x'=4,'c'=2] {'z'}, dimensions={0} | all-to-all | bytes 3145728 | tf_op jit(solution)/shard_map/all_to_all | solution.py:169
  101.9 0.0 all-gather.3.cloned.1.call-done
  101.9 3.4 %shard_map.59 = (bf16[32,16,128]{2,1,0:T(8,128)(2,1)S(1)}, bf16[32,16,128]{2,1,0:T(8,128)(2,1)S(1)}) custom-call(s32[1]{0:T(128)} %bitcast.2.core_ref, bf16[8,64,1536]{2,1,0:T(8,128)(2,1)S(1)} %all_to_all.16.parts_ref, bf16[8,1536,128]{2,1,0:T(8,128)(2,1)} %bitcast.6), custom_call_target="tpu_custom_call" | custom-call | tf_op jit(solution)/shard_map/pallas_call | solution.py:27
  105.2 2.4 %collective-permute-start.2 = (bf16[32,16,128]{2,1,0:T(8,128)(2,1)S(1)}, bf16[32,16,128]{2,1,0:T(8,128)(2,1)S(1)}, u32[]{:S(2)}, u32[]{:S(2)}) collective-permute-start(bf16[32,16,128]{2,1,0:T(8,128)(2,1)S(1)} %get-tuple-element.12), channel_id=1, source_target_pairs={{0,1},{1,0},{2,3},{3,2},{4,5},{5,4},{6,7},{7,6},{8,9},{9,8},{10,11... | collective-permute-start | bytes 393224 | tf_op jit(solution)/shard_map/ppermute | solution.py:211
  107.6 1.0 collective-permute-done.2.recv_ref
  108.6 0.8 shard_map.60
  109.3 6.1 %all-to-all-start.2 = ((bf16[32,16,128]{2,1,0:T(8,128)(2,1)}), bf16[32,16,128]{2,1,0:T(8,128)(2,1)S(1)}, u32[]{:S(2)}, u32[]{:S(2)}) async-start(bf16[32,16,128]{2,1,0:T(8,128)(2,1)} %shard_map.60), calls=%async_computation.2 | async-start | bytes 262144 | tf_op jit(solution)/shard_map/all_to_all | solution.py:169
  116.1 0.1 shard_map.56.count_ref
  116.2 8.6 %all-to-all-done.2.in_ref = bf16[32,16,128]{2,1,0:T(8,128)(2,1)S(1)} async-done(((bf16[32,16,128]{2,1,0:T(8,128)(2,1)}), bf16[32,16,128]{2,1,0:T(8,128)(2,1)S(1)}, u32[]{:S(2)}, u32[]{:S(2)}) %all-to-all-start.2) | async-done | bytes 131104 | tf_op jit(solution)/shard_map/all_to_all | solution.py:169
  124.8 0.8 shard_map.61
Async XLA Ops:
  6.5 95.3 %all-gather.3.cloned.1.call-start = ((), (), s32[]{:S(2)}) async-start(), calls=%async_computation.3 | async-start | bytes 3538944 | tf_op jit(solution)/shard_map/all_gather | solution.py:174
  8.3 12.6 %collective-permute-start = (bf16[64,128]{1,0:T(8,128)(2,1)S(1)}, bf16[64,128]{1,0:T(8,128)(2,1)S(1)}, u32[]{:S(2)}, u32[]{:S(2)}) collective-permute-start(bf16[64,128]{1,0:T(8,128)(2,1)S(1)} %shard_map.55), channel_id=1, source_target_pairs={{0,32},{1,33},{2,34},{3,35},{4,36},{5,37},{6,38},{7,39},{8,96},{9,... | collective-permute-start | bytes 49160 | tf_op jit(solution)/shard_map/ppermute | solution.py:176
  45.5 7.4 %collective-permute-start.1 = (bf16[32,64,128]{2,1,0:T(8,128)(2,1)S(1)}, bf16[32,64,128]{2,1,0:T(8,128)(2,1)S(1)}, u32[]{:S(2)}, u32[]{:S(2)}) collective-permute-start(bf16[32,64,128]{2,1,0:T(8,128)(2,1)S(1)} %all_to_all.15.own_ref), channel_id=1, source_target_pairs={{0,1},{1,0},{2,3},{3,2},{4,5},{5,4},{6,7},{7,6},{8,9},{9,8},{10,11... | collective-permute-start | bytes 1572872 | tf_op jit(solution)/shard_map/ppermute | solution.py:179
  105.2 3.3 %collective-permute-start.2 = (bf16[32,16,128]{2,1,0:T(8,128)(2,1)S(1)}, bf16[32,16,128]{2,1,0:T(8,128)(2,1)S(1)}, u32[]{:S(2)}, u32[]{:S(2)}) collective-permute-start(bf16[32,16,128]{2,1,0:T(8,128)(2,1)S(1)} %get-tuple-element.12), channel_id=1, source_target_pairs={{0,1},{1,0},{2,3},{3,2},{4,5},{5,4},{6,7},{7,6},{8,9},{9,8},{10,11... | collective-permute-start | bytes 393224 | tf_op jit(solution)/shard_map/ppermute | solution.py:211
  109.3 15.5 %all-to-all-start.2 = ((bf16[32,16,128]{2,1,0:T(8,128)(2,1)}), bf16[32,16,128]{2,1,0:T(8,128)(2,1)S(1)}, u32[]{:S(2)}, u32[]{:S(2)}) async-start(bf16[32,16,128]{2,1,0:T(8,128)(2,1)} %shard_map.60), calls=%async_computation.2 | async-start | bytes 262144 | tf_op jit(solution)/shard_map/all_to_all | solution.py:169
Sparse Core Ops, SparseCore 0:
  9.4 53.6 all-gather.2

commit v9 on v8

--- a/solution.py
+++ b/solution.py
@@ -43,15 +43,12 @@
     return lax.broadcasted_iota(jnp.int32, shape, axis)
 
 
-def select_kernel(index_ref, hidden_ref, out_ref):
+def select_kernel(index_ref, hidden_ref, count_ref, out_ref, live_ref):
+    live_ref[...] = jnp.broadcast_to(count_ref[...], (8, 128))
     chosen = jnp.where(iota((256, 64), 0) == index_ref[...], 1.0, 0.0).astype(BF16)
     out_ref[...] = lax.dot_general(
         chosen, hidden_ref[...], (((0,), (0,)), ((), ())), preferred_element_type=F32
     ).astype(BF16)
-
-
-def live_kernel(count_ref, out_ref):
-    out_ref[...] = jnp.broadcast_to(count_ref[...], (8, 128))
 
 
 def hold_kernel(head_ref, out_ref, sem):
@@ -169,12 +166,18 @@
         return lax.all_to_all(v, axes, 0, 0, tiled=True)
 
     core = lax.axis_index("c").astype(jnp.int32).reshape(1)
-    owned = call(select_kernel, ((64, 128), BF16), [OUTER, OUTER], keep_index.reshape(1, 64), hidden)
-    late_counts, owned = lax.optimization_barrier((counts, owned))
-    basis = lax.all_gather(vocab_basis, "z")
+    owned, live = call(
+        select_kernel,
+        [((64, 128), BF16), ((8, 128), jnp.int32)],
+        [OUTER, OUTER, OUTER],
+        keep_index.reshape(1, 64),
+        hidden,
+        counts.reshape(1, 1),
+    )
+    late_basis, owned = lax.optimization_barrier((vocab_basis, owned))
+    basis = lax.all_gather(late_basis, "z")
     pairs = [((z * 8 + y) * 8 + k, (y * 8 + (z + 4) % 8) * 8 + k) for z in range(8) for y in range(8) for k in range(8)]
     moved = lax.ppermute(owned, ("z", "y", "x", "c"), pairs)
-    live = call(live_kernel, ((8, 128), jnp.int32), [OUTER], late_counts.reshape(1, 1))
     mine = exchange(jnp.broadcast_to(moved[None], (32, 64, 128)), ("y", "x"))
     theirs = lax.ppermute(mine, "c", [(0, 1), (1, 0)])
     held = call(

time: 133 us -> 132 us (level)
  blocking collectives: 71.6 us -> 87 us
  waiting for transfers between devices: 14.6 us -> 5.28 us
  starting transfers between devices: 22.3 us -> 16.1 us
    all_to_all x2 -> x3, blocking collectives: 71.6 us -> 87 us  [exchange(): return lax.all_to_all(v, axes, 0, 0, tiled=True)]
    all_to_all x1 -> x0, waiting for transfers between devices: 8.63 us -> none  [exchange(): return lax.all_to_all(v, axes, 0, 0, tiled=True)]
    all_to_all x1 -> x0, starting transfers between devices: 6.14 us -> none  [exchange(): return lax.all_to_all(v, axes, 0, 0, tiled=True)]
    pallas_call x7 -> x6, Pallas kernels: 9.71 us -> 8.99 us  [call(): pl.pallas_call(kernel, out_shape=shapes, in_specs=in_specs, out_specs=[VM...]
  transfers between devices with their start and end apart: 5 -> 4, of which waited for: 3 -> 2; matrix products, arithmetic and copies ran while one was open for 0% -> 0% of each run, Pallas kernels for 4% -> 3%
where the time goes in v9:
time: 132 us
  blocking collectives  87 us (66%)
  starting transfers between devices  16.1 us (12%)
  between operations  14.1 us (11%)
  Pallas kernels  8.99 us (7%)
  waiting for transfers between devices  5.28 us (4%)
    all_to_all x3, blocking collectives, exchange(): return lax.all_to_all(v, axes, 0, 0, tiled=True)  87 us
    pallas_call x6, Pallas kernels, call(): pl.pallas_call(kernel, out_shape=shapes, in_specs=in_specs, out_specs=[VM...  8.99 us
    ppermute x1, starting transfers between devices, shards(): moved = lax.ppermute(owned, ('z', 'y', 'x', 'c'), pairs)  8.27 us
    ppermute x1, starting transfers between devices, shards(): theirs = lax.ppermute(mine, 'c', [(0, 1), (1, 0)])  5.47 us
    ppermute x1, waiting for transfers between devices, shards(): moved = lax.ppermute(owned, ('z', 'y', 'x', 'c'), pairs)  4.3 us
  transfers between devices with their start and end apart: 4, of which 2 were waited for; matrix products, arithmetic and copies ran while one was open for 0% of the time, Pallas kernels for 3%

profile of v9, /device:TPU:1, one launch (start us, length us, event | category | flops | bytes accessed | tf_op | source)
XLA Modules:
  0.0 131.6 jit_solution(195862639803001846)
XLA Ops:
  6.5 0.0 all-gather.3.cloned.1.call-start
  7.2 1.0 shard_map.55
  8.2 0.0 all-gather.3.cloned.1.call-update
  8.3 8.3 %collective-permute-start = (bf16[64,128]{1,0:T(8,128)(2,1)S(1)}, bf16[64,128]{1,0:T(8,128)(2,1)S(1)}, u32[]{:S(2)}, u32[]{:S(2)}) collective-permute-start(bf16[64,128]{1,0:T(8,128)(2,1)S(1)} %get-tuple-element.13), channel_id=1, source_target_pairs={{0,32},{1,33},{2,34},{3,35},{4,36},{5,37},{6,38},{7,39},{8,96},{9,... | collective-permute-start | bytes 49160 | tf_op jit(solution)/shard_map/ppermute | solution.py:180
  16.5 4.3 %collective-permute-done = bf16[64,128]{1,0:T(8,128)(2,1)S(1)} collective-permute-done((bf16[64,128]{1,0:T(8,128)(2,1)S(1)}, bf16[64,128]{1,0:T(8,128)(2,1)S(1)}, u32[]{:S(2)}, u32[]{:S(2)}) %collective-permute-start) | collective-permute-done | bytes 16416 | tf_op jit(solution)/shard_map/ppermute | solution.py:180
  20.8 0.1 broadcast_in_dim.2
  20.9 24.5 %all_to_all.15.own_ref = bf16[32,64,128]{2,1,0:T(8,128)(2,1)S(1)} all-to-all(bf16[32,64,128]{2,1,0:T(8,128)(2,1)S(1)} %broadcast_in_dim.2), channel_id=1, replica_groups=mesh['z'=8,'y'=8,'x'=4,'c'=2] {'y','x'}, dimensions={0} | all-to-all | bytes 1048576 | tf_op jit(solution)/shard_map/all_to_all | solution.py:166
  45.4 5.5 %collective-permute-start.1 = (bf16[32,64,128]{2,1,0:T(8,128)(2,1)S(1)}, bf16[32,64,128]{2,1,0:T(8,128)(2,1)S(1)}, u32[]{:S(2)}, u32[]{:S(2)}) collective-permute-start(bf16[32,64,128]{2,1,0:T(8,128)(2,1)S(1)} %all_to_all.15.own_ref), channel_id=1, source_target_pairs={{0,1},{1,0},{2,3},{3,2},{4,5},{5,4},{6,7},{7,6},{8,9},{9,8},{10,11... | collective-permute-start | bytes 1572872 | tf_op jit(solution)/shard_map/ppermute | solution.py:182
  50.9 1.9 %shard_map.56.head_ref = bf16[1024,1536]{1,0:T(8,128)(2,1)S(1)} custom-call(bf16[1024,1536]{1,0:T(8,128)(2,1)} %head_ref.1), custom_call_target="tpu_custom_call" | custom-call | tf_op jit(solution)/shard_map/pallas_call | solution.py:27
  52.8 0.0 collective-permute-done.1.other_ref
  52.9 1.8 %shard_map.57 = bf16[8,64,1536]{2,1,0:T(8,128)(2,1)S(1)} custom-call(s32[1]{0:T(128)} %bitcast.2.core_ref, bf16[32,64,128]{2,1,0:T(8,128)(2,1)S(1)} %all_to_all.15.own_ref, bf16[32,64,128]{2,1,0:T(8,128)(2,1)S(1)} %collective-permute-done.1.other_ref, bf16[1024,1536]{1,0:T(8,128)(2,1)S(1)} %shard_map.56.head_ref), custom_call_target="tpu_custom_call" | custom-call | tf_op jit(solution)/shard_map/pallas_call | solution.py:27
  54.7 47.2 %all_to_all.16.parts_ref = bf16[8,64,1536]{2,1,0:T(8,128)(2,1)S(1)} all-to-all(bf16[8,64,1536]{2,1,0:T(8,128)(2,1)S(1)} %shard_map.57), channel_id=1, replica_groups=mesh['z'=8,'y'=8,'x'=4,'c'=2] {'z'}, dimensions={0} | all-to-all | bytes 3145728 | tf_op jit(solution)/shard_map/all_to_all | solution.py:166
  101.8 0.0 all-gather.3.cloned.1.call-done
  101.8 3.4 %shard_map.58 = (bf16[32,16,128]{2,1,0:T(8,128)(2,1)S(1)}, bf16[32,16,128]{2,1,0:T(8,128)(2,1)S(1)}) custom-call(s32[1]{0:T(128)} %bitcast.2.core_ref, bf16[8,64,1536]{2,1,0:T(8,128)(2,1)S(1)} %all_to_all.16.parts_ref, bf16[8,1536,128]{2,1,0:T(8,128)(2,1)} %bitcast.6), custom_call_target="tpu_custom_call" | custom-call | tf_op jit(solution)/shard_map/pallas_call | solution.py:27
  105.2 2.4 %collective-permute-start.2 = (bf16[32,16,128]{2,1,0:T(8,128)(2,1)S(1)}, bf16[32,16,128]{2,1,0:T(8,128)(2,1)S(1)}, u32[]{:S(2)}, u32[]{:S(2)}) collective-permute-start(bf16[32,16,128]{2,1,0:T(8,128)(2,1)S(1)} %get-tuple-element.16), channel_id=1, source_target_pairs={{0,1},{1,0},{2,3},{3,2},{4,5},{5,4},{6,7},{7,6},{8,9},{9,8},{10,11... | collective-permute-start | bytes 393224 | tf_op jit(solution)/shard_map/ppermute | solution.py:214
  107.6 1.0 collective-permute-done.2.recv_ref
  108.5 0.1 shard_map.59
  108.6 15.3 %all_to_all.17.in_ref = bf16[32,16,128]{2,1,0:T(8,128)(2,1)S(1)} all-to-all(bf16[32,16,128]{2,1,0:T(8,128)(2,1)S(1)} %shard_map.59), channel_id=1, replica_groups=mesh['z'=8,'y'=8,'x'=4,'c'=2] {'y','x'}, dimensions={0} | all-to-all | bytes 262144 | tf_op jit(solution)/shard_map/all_to_all | solution.py:166
  124.0 0.8 shard_map.60
Async XLA Ops:
  6.5 95.3 %all-gather.3.cloned.1.call-start = ((), (), s32[]{:S(2)}) async-start(), calls=%async_computation.3 | async-start | bytes 3538944 | tf_op jit(solution)/shard_map/all_gather | solution.py:178
  8.3 12.6 %collective-permute-start = (bf16[64,128]{1,0:T(8,128)(2,1)S(1)}, bf16[64,128]{1,0:T(8,128)(2,1)S(1)}, u32[]{:S(2)}, u32[]{:S(2)}) collective-permute-start(bf16[64,128]{1,0:T(8,128)(2,1)S(1)} %get-tuple-element.13), channel_id=1, source_target_pairs={{0,32},{1,33},{2,34},{3,35},{4,36},{5,37},{6,38},{7,39},{8,96},{9,... | collective-permute-start | bytes 49160 | tf_op jit(solution)/shard_map/ppermute | solution.py:180
  45.4 7.4 %collective-permute-start.1 = (bf16[32,64,128]{2,1,0:T(8,128)(2,1)S(1)}, bf16[32,64,128]{2,1,0:T(8,128)(2,1)S(1)}, u32[]{:S(2)}, u32[]{:S(2)}) collective-permute-start(bf16[32,64,128]{2,1,0:T(8,128)(2,1)S(1)} %all_to_all.15.own_ref), channel_id=1, source_target_pairs={{0,1},{1,0},{2,3},{3,2},{4,5},{5,4},{6,7},{7,6},{8,9},{9,8},{10,11... | collective-permute-start | bytes 1572872 | tf_op jit(solution)/shard_map/ppermute | solution.py:182
  105.2 3.3 %collective-permute-start.2 = (bf16[32,16,128]{2,1,0:T(8,128)(2,1)S(1)}, bf16[32,16,128]{2,1,0:T(8,128)(2,1)S(1)}, u32[]{:S(2)}, u32[]{:S(2)}) collective-permute-start(bf16[32,16,128]{2,1,0:T(8,128)(2,1)S(1)} %get-tuple-element.16), channel_id=1, source_target_pairs={{0,1},{1,0},{2,3},{3,2},{4,5},{5,4},{6,7},{7,6},{8,9},{9,8},{10,11... | collective-permute-start | bytes 393224 | tf_op jit(solution)/shard_map/ppermute | solution.py:214
Sparse Core Ops, SparseCore 0:
  9.4 53.6 all-gather.2
